TPU v7x, 32 devices: a whole 2x2x4 slice. The times are simulated.
32 devices in a mesh: lon: 8 (over z, x), lat: 4 (over y, core).
Axes of the slice: x: 2, y: 2, z: 4, core: 2. Of those that a mesh axis runs over, the one named last changes fastest.
Arguments:
- control_fields: float32 [2, 4, 544, 1536], P(None, None, 'lon', 'lat'), may hold values from -4 to 4
- unexplained_elevation: float32 [544, 1536], P('lon', 'lat'), may hold values from -6 to 6
- diffusivity: float32 [544, 1536], P('lon', 'lat'), may hold values from 0.15 to 0.49
- depth_levels: int32 [544, 1536], P('lon', 'lat'), may hold values from 0 to 4
- fold_partner: int32 [544], replicated, may hold values from 0 to 543, as said below
- prior_sigmas: float32 [2, 4], replicated, may hold values from 0.5 to 2
- haline_thermal_ratio: float32 [544, 1536], P('lon', 'lat'), may hold values from -0.6 to 0.6
- expansion_coefficients: float32 [2, 4], replicated, may hold values from -3 to 3
Outputs:
- state_fields: float32 [2, 4, 544, 1536], P(None, None, 'lon', 'lat')
- sea_height: float32 [544, 1536], P('lon', 'lat')
Inputs may be any that keep to these rules, and one draw needn't show every extreme that they name: `fold_partner`: column i's fold partner lies in the block of 68 columns with block index (8 - (i div 68)) mod (8); within one block the partners are distinct.
All inputs are finite; a program needn't handle non-finite values.
Results may differ from a plain program's by a relative error of at most 0.0003.
Values sent between devices are 32-bit elements; how exact they have to be, the bound alone decides.
A program may use at most 64 MiB of HBM per device.

v0:
```python
import jax
import jax.numpy as jnp
from jax import lax
from jax.sharding import PartitionSpec as P

PASSES = 4


def extended_2(block, sides, width, periodic):
    for axis, dim in sides:
        count = lax.axis_size(axis)
        forward = [(i, i + 1) for i in range(count - 1)]
        if periodic:
            forward.append((count - 1, 0))
        backward = [(target, source) for source, target in forward]
        low = lax.ppermute(
            lax.slice_in_dim(block, block.shape[dim] - width, None, axis=dim), axis, forward
        )
        high = lax.ppermute(lax.slice_in_dim(block, 0, width, axis=dim), axis, backward)
        block = jnp.concatenate([low, block, high], axis=dim)
    return block


def conductances(coefficients, level_values):
    kappa_padded = coefficients[0]
    wet_padded = (level_values < coefficients[1][None]).astype(jnp.float32)
    row_kappa = kappa_padded[:, 1:-1]
    row_wet = wet_padded[:, :, 1:-1]
    along_lon = (row_kappa[:-1] * row_kappa[1:])[None] * row_wet[:, :-1] * row_wet[:, 1:]
    column_kappa = kappa_padded[1:-1]
    column_wet = wet_padded[:, 1:-1]
    along_lat = (
        (column_kappa[:, :-1] * column_kappa[:, 1:])[None]
        * column_wet[:, :, :-1]
        * column_wet[:, :, 1:]
    )
    return (along_lon[:, 1:], along_lon[:, :-1], along_lat[:, :, 1:], along_lat[:, :, :-1])


def diffuse_once(padded, faces, levels_count):
    east_face, west_face, north_face, south_face = faces
    grid = padded.reshape(2, levels_count, padded.shape[1], padded.shape[2])
    centre = grid[:, :, 1:-1, 1:-1]
    result = (
        centre
        + east_face * (grid[:, :, 2:, 1:-1] - centre)
        + west_face * (grid[:, :, :-2, 1:-1] - centre)
        + north_face * (grid[:, :, 1:-1, 2:] - centre)
        + south_face * (grid[:, :, 1:-1, :-2] - centre)
    )
    return result.reshape(2 * levels_count, padded.shape[1] - 2, padded.shape[2] - 2)


def local(
    control_fields,
    unexplained_elevation,
    diffusivity,
    depth_levels,
    fold_partner,
    prior_sigmas,
    haline_thermal_ratio,
    expansion_coefficients,
):
    levels_count = control_fields.shape[1]
    lon_cells = control_fields.shape[2]
    lat_cells = control_fields.shape[3]
    stacked_rows = 2 * levels_count
    lat_devices = lax.axis_size("lat")
    lon_place = lax.axis_index("lon")
    at_top = (lax.axis_index("lat") == lat_devices - 1).astype(jnp.float32)
    depth_float = depth_levels.astype(jnp.float32)
    level_values = jnp.arange(levels_count, dtype=jnp.float32)[:, None, None]
    wet_cells = (level_values < depth_float[None]).astype(jnp.float32)
    masked = (control_fields * wet_cells[None]).reshape(stacked_rows, lon_cells, lat_cells)
    current = jnp.concatenate([masked, diffusivity[None], depth_float[None]], axis=0)
    margin = 1
    own_columns = lon_place * lon_cells + jnp.arange(lon_cells, dtype=jnp.int32)
    own_partners = fold_partner[own_columns]
    faces = None
    for repeat in range(PASSES):
        extended = extended_2(current, (("lon", 1),), 1, True)
        top_rows = extended[:, margin : margin + lon_cells, lat_cells - 1]
        every_top = lax.all_gather(top_rows, "lon", axis=1, tiled=True)
        folded = jnp.take(every_top, own_partners, axis=1)
        folded = jnp.concatenate(
            [jnp.zeros_like(folded[:, :1]), folded, jnp.zeros_like(folded[:, :1])], axis=1
        )
        padded = extended_2(extended, (("lat", 2),), 1, False)
        padded = padded.at[:, :, lat_cells + 1].add(at_top * folded)
        if repeat == 0:
            faces = conductances(padded[stacked_rows:], level_values)
            padded = padded[:stacked_rows]
            extended = extended[:stacked_rows]
        inner = diffuse_once(padded, faces, levels_count)
        current = inner
    assembled_output = current
    assembled_output = assembled_output.reshape(2, levels_count, lon_cells, lat_cells)
    thermal_grid = prior_sigmas[0][:, None, None] * assembled_output[0]
    saltiness_grid = (
        prior_sigmas[1][:, None, None] * assembled_output[1]
        + haline_thermal_ratio[None] * thermal_grid
    )
    ocean_elevation = unexplained_elevation + jnp.sum(
        expansion_coefficients[0][:, None, None] * thermal_grid
        + expansion_coefficients[1][:, None, None] * saltiness_grid,
        axis=0,
    )
    return (jnp.stack([thermal_grid, saltiness_grid]), ocean_elevation)


def solution(mesh):
    return jax.shard_map(
        local,
        mesh=mesh,
        in_specs=(
            P(None, None, "lon", "lat"),
            P("lon", "lat"),
            P("lon", "lat"),
            P("lon", "lat"),
            P(),
            P(),
            P("lon", "lat"),
            P(),
        ),
        out_specs=(P(None, None, "lon", "lat"), P("lon", "lat")),
        check_vma=False,
    )
```

profile of v0, /device:TPU:1, one launch (start us, length us, event | category | flops | bytes accessed | tf_op | source)
XLA Modules:
  0.0 226.4 jit_solution(13621705072636186898)
XLA Ops:
  0.6 0.9 fusion.55
  1.7 1.3 broadcast_multiply_fusion
  3.1 2.1 collective-permute-start
  5.2 3.1 %collective-permute-start.1 = (f32[10,1,384]{2,1,0:T(1,128)S(1)}, f32[10,1,384]{2,1,0:T(1,128)S(1)}, u32[]{:S(2)}, u32[]{:S(2)}) collective-permute-start(f32[10,1,384]{2,1,0:T(1,128)S(1)} %get-tuple-element.74), channel_id=1, source_target_pairs={{4,0},{8,4},{12,8},{16,12},{20,16},{24,20},{28,24},{0,28},{5,1},{9... | collective-permute-start | bytes 46088 | tf_op jit(solution)/shard_map/ppermute | solution.py:19
  8.3 1.0 gather_fusion
  9.5 0.5 copy.175
  10.0 24.6 %all-gather = f32[10,544,1]{0,2,1:T(1,128)S(1)} all-gather(f32[10,68,1]{0,2,1:T(1,128)S(1)} %copy.175), channel_id=2, replica_groups=mesh['lon'=8,'lat'=4] {'lon'}, dimensions={1}, use_global_device_ids=true | all-gather | bytes 24480 | tf_op jit(solution)/shard_map/all_gather | solution.py:83
  34.6 0.6 gather_fusion.1
  35.7 9.0 %collective-permute-start.3 = (f32[10,70,1]{1,2,0:T(1,128)S(1)}, f32[10,70,1]{1,2,0:T(1,128)S(1)}, u32[]{:S(2)}, u32[]{:S(2)}) collective-permute-start(f32[10,70,1]{1,2,0:T(1,128)S(1)} %copy.174), channel_id=1, source_target_pairs={{1,0},{2,1},{3,2},{5,4},{6,5},{7,6},{9,8},{10,9},{11,10},{13,12},{... | collective-permute-start | bytes 8408 | tf_op jit(solution)/shard_map/ppermute | solution.py:19
  44.8 3.3 %collective-permute-start.2 = (f32[10,70,1]{2,1,0:T(8,128)S(1)}, f32[10,70,1]{2,1,0:T(8,128)}, u32[]{:S(2)}, u32[]{:S(2)}) collective-permute-start(f32[10,70,1]{2,1,0:T(8,128)S(1)} %get-tuple-element.71), channel_id=1, source_target_pairs={{0,1},{1,2},{2,3},{4,5},{5,6},{6,7},{8,9},{9,10},{10,11},{12,13},{... | collective-permute-start | bytes 8408 | tf_op jit(solution)/shard_map/ppermute | solution.py:16
  48.7 3.9 %collective-permute-done.2 = f32[10,70,1]{2,1,0:T(8,128)} collective-permute-done((f32[10,70,1]{2,1,0:T(8,128)S(1)}, f32[10,70,1]{2,1,0:T(8,128)}, u32[]{:S(2)}, u32[]{:S(2)}) %collective-permute-start.2) | collective-permute-done | bytes 2832 | tf_op jit(solution)/shard_map/ppermute | solution.py:16
  52.5 1.7 pad_maximum_fusion.3
  54.2 3.6 %scatter-add.14 = f32[10,70,386]{2,1,0:T(8,128)S(1)} dynamic-update-slice(f32[10,70,386]{2,1,0:T(8,128)S(1)} %pad_maximum_fusion.3, f32[10,70,1]{2,1,0:T(8,128)S(1)} %copy.148, s32[]{:T(128)} %constant.128.clone.1, s32[]{:T(128)} %constant.128.clone.1, s32[]{:T(128)} %constant.132.clone.1) | dynamic-update-slice | bytes 5604 | tf_op jit(solution)/shard_map/scatter-add | solution.py:89
  58.4 0.3 slice_multiply_fusion.2
  58.7 0.3 slice_multiply_fusion
  59.2 1.0 fusion.25
  60.4 1.5 collective-permute-start.5
  62.1 0.6 copy.152
  62.7 0.5 copy.154
  63.2 24.9 %all-gather.1 = f32[8,544,1]{0,2,1:T(1,128)S(1)} all-gather(f32[8,68,1]{0,2,1:T(1,128)S(1)} %copy.154), channel_id=3, replica_groups=mesh['lon'=8,'lat'=4] {'lon'}, dimensions={1}, use_global_device_ids=true | all-gather | bytes 19584 | tf_op jit(solution)/shard_map/all_gather | solution.py:83
  88.1 0.6 gather_fusion.2
  88.7 0.6 copy.151
  89.3 1.7 copy.153
  91.0 0.8 pad_maximum_fusion.28
  91.8 11.0 %collective-permute-start.6 = (f32[8,70,1]{1,0,2:T(8,128)S(1)}, f32[8,70,1]{1,0,2:T(8,128)S(1)}, u32[]{:S(2)}, u32[]{:S(2)}) collective-permute-start(f32[8,70,1]{1,0,2:T(8,128)S(1)} %get-tuple-element.67), channel_id=1, source_target_pairs={{0,1},{1,2},{2,3},{4,5},{5,6},{6,7},{8,9},{9,10},{10,11},{12,13},{... | collective-permute-start | bytes 6728 | tf_op jit(solution)/shard_map/ppermute | solution.py:16
  102.8 1.9 collective-permute-start.7
  104.8 2.8 %collective-permute-done.7 = f32[8,70,1]{1,0,2:T(8,128)S(1)} collective-permute-done((f32[8,70,1]{1,0,2:T(8,128)S(1)}, f32[8,70,1]{1,0,2:T(8,128)S(1)}, u32[]{:S(2)}, u32[]{:S(2)}) %collective-permute-start.7) | collective-permute-done | bytes 2272 | tf_op jit(solution)/shard_map/ppermute | solution.py:19
  107.7 3.5 %pad_maximum_fusion = f32[8,70,386]{1,0,2:T(8,128)} fusion(f32[8,70,1]{1,0,2:T(8,128)S(1)} %collective-permute-done.7, f32[8,1,384]{1,0,2:T(8,128)} %copy.153, f32[8,68,384]{1,0,2:T(8,128)S(1)} %copy.152, f32[8,1,384]{1,0,2:T(8,128)S(1)} %copy.151, f32[8,70,1]{1,0,2:T(8,128)S(1)} %collective-permute-done.6), kind=kLoop, calls=%fused_computation.5 | loop fusion | flops 864640 | bytes 1729280 | tf_op jit(solution)/shard_map/concatenate | solution.py:20
  111.2 0.7 fusion.41
  111.8 2.1 copy.156
  114.0 1.0 fusion.17
  115.0 1.5 collective-permute-start.8
  116.5 2.8 %collective-permute-start.9 = (f32[8,1,384]{2,0,1:T(8,128)S(1)}, f32[8,1,384]{2,0,1:T(8,128)S(1)}, u32[]{:S(2)}, u32[]{:S(2)}) collective-permute-start(f32[8,1,384]{2,0,1:T(8,128)S(1)} %copy.158), channel_id=1, source_target_pairs={{4,0},{8,4},{12,8},{16,12},{20,16},{24,20},{28,24},{0,28},{5,1},{9... | collective-permute-start | bytes 36872 | tf_op jit(solution)/shard_map/ppermute | solution.py:19
  119.4 1.8 copy.160
  121.3 0.5 copy.162
  121.7 25.0 %all-gather.2 = f32[8,544,1]{0,2,1:T(1,128)S(1)} all-gather(f32[8,68,1]{0,2,1:T(1,128)S(1)} %copy.162), channel_id=4, replica_groups=mesh['lon'=8,'lat'=4] {'lon'}, dimensions={1}, use_global_device_ids=true | all-gather | bytes 19584 | tf_op jit(solution)/shard_map/all_gather | solution.py:83
  146.7 0.6 gather_fusion.3
  147.3 0.6 copy.159
  148.0 1.7 copy.161
  149.6 0.8 pad_maximum_fusion.25
  150.4 8.4 %collective-permute-start.10 = (f32[8,70,1]{1,0,2:T(8,128)S(1)}, f32[8,70,1]{1,0,2:T(8,128)S(1)}, u32[]{:S(2)}, u32[]{:S(2)}) collective-permute-start(f32[8,70,1]{1,0,2:T(8,128)S(1)} %get-tuple-element.65), channel_id=1, source_target_pairs={{0,1},{1,2},{2,3},{4,5},{5,6},{6,7},{8,9},{9,10},{10,11},{12,13},{... | collective-permute-start | bytes 6728 | tf_op jit(solution)/shard_map/ppermute | solution.py:16
  158.8 1.9 collective-permute-start.11
  160.9 2.8 %collective-permute-done.11 = f32[8,70,1]{1,0,2:T(8,128)S(1)} collective-permute-done((f32[8,70,1]{1,0,2:T(8,128)S(1)}, f32[8,70,1]{1,0,2:T(8,128)S(1)}, u32[]{:S(2)}, u32[]{:S(2)}) %collective-permute-start.11) | collective-permute-done | bytes 2272 | tf_op jit(solution)/shard_map/ppermute | solution.py:19
  163.7 3.5 %pad_maximum_fusion.1 = f32[8,70,386]{1,0,2:T(8,128)} fusion(f32[8,70,1]{1,0,2:T(8,128)S(1)} %collective-permute-done.11, f32[8,1,384]{1,0,2:T(8,128)} %copy.161, f32[8,68,384]{1,0,2:T(8,128)S(1)} %copy.160, f32[8,1,384]{1,0,2:T(8,128)S(1)} %copy.159, f32[8,70,1]{1,0,2:T(8,128)S(1)} %collective-permute-done.10), kind=kLoop, calls=%fused_computation.6 | loop fusion | flops 864640 | bytes 1729280 | tf_op jit(solution)/shard_map/concatenate | solution.py:20
  167.2 0.7 fusion.44
  167.8 2.1 copy.164
  170.0 1.0 fusion.9
  171.1 1.5 collective-permute-start.13
  172.8 1.8 copy.168
  174.6 0.5 copy.170
  175.0 24.9 %all-gather.3 = f32[8,544,1]{0,2,1:T(1,128)S(1)} all-gather(f32[8,68,1]{0,2,1:T(1,128)S(1)} %copy.170), channel_id=5, replica_groups=mesh['lon'=8,'lat'=4] {'lon'}, dimensions={1}, use_global_device_ids=true | all-gather | bytes 19584 | tf_op jit(solution)/shard_map/all_gather | solution.py:83
  199.9 0.6 gather_fusion.4
  200.6 0.6 copy.167
  201.2 1.7 copy.169
  202.8 0.8 pad_maximum_fusion.22
  203.6 8.4 %collective-permute-start.14 = (f32[8,70,1]{1,0,2:T(8,128)S(1)}, f32[8,70,1]{1,0,2:T(8,128)S(1)}, u32[]{:S(2)}, u32[]{:S(2)}) collective-permute-start(f32[8,70,1]{1,0,2:T(8,128)S(1)} %get-tuple-element.63), channel_id=1, source_target_pairs={{0,1},{1,2},{2,3},{4,5},{5,6},{6,7},{8,9},{9,10},{10,11},{12,13},{... | collective-permute-start | bytes 6728 | tf_op jit(solution)/shard_map/ppermute | solution.py:16
  212.0 1.9 collective-permute-start.15
  214.1 2.8 %collective-permute-done.15 = f32[8,70,1]{1,0,2:T(8,128)S(1)} collective-permute-done((f32[8,70,1]{1,0,2:T(8,128)S(1)}, f32[8,70,1]{1,0,2:T(8,128)S(1)}, u32[]{:S(2)}, u32[]{:S(2)}) %collective-permute-start.15) | collective-permute-done | bytes 2272 | tf_op jit(solution)/shard_map/ppermute | solution.py:19
  216.9 3.5 %pad_maximum_fusion.2 = f32[8,70,386]{1,0,2:T(8,128)} fusion(f32[8,70,1]{1,0,2:T(8,128)S(1)} %collective-permute-done.15, f32[8,1,384]{1,0,2:T(8,128)} %copy.169, f32[8,68,384]{1,0,2:T(8,128)S(1)} %copy.168, f32[8,1,384]{1,0,2:T(8,128)S(1)} %copy.167, f32[8,70,1]{1,0,2:T(8,128)S(1)} %collective-permute-done.14), kind=kLoop, calls=%fused_computation.7 | loop fusion | flops 864640 | bytes 1729280 | tf_op jit(solution)/shard_map/concatenate | solution.py:20
  220.4 0.7 fusion.47
  221.1 2.1 copy.172
  223.2 1.0 fusion.1
  224.5 1.1 copy.173
  225.8 0.7 add.169
  (111 shorter events, 3.7 us)
Async XLA Ops:
  0.6 7.7 %copy-start = (s32[544]{0:T(1024)S(1)}, s32[544]{0:T(1024)}, u32[]{:S(2)}) copy-start(s32[544]{0:T(1024)} %param.22) | copy-start | bytes 6532
  1.7 1.4 copy-start.19
  3.1 32.2 %collective-permute-start = (f32[10,1,384]{2,1,0:T(1,128)S(1)}, f32[10,1,384]{2,1,0:T(1,128)S(1)}, u32[]{:S(2)}, u32[]{:S(2)}) collective-permute-start(f32[10,1,384]{2,1,0:T(1,128)S(1)} %get-tuple-element.73), channel_id=1, source_target_pairs={{0,4},{4,8},{8,12},{12,16},{16,20},{20,24},{24,28},{28,0},{1,5},{5... | collective-permute-start | bytes 46088 | tf_op jit(solution)/shard_map/ppermute | solution.py:16
  5.2 30.1 %collective-permute-start.1 = (f32[10,1,384]{2,1,0:T(1,128)S(1)}, f32[10,1,384]{2,1,0:T(1,128)S(1)}, u32[]{:S(2)}, u32[]{:S(2)}) collective-permute-start(f32[10,1,384]{2,1,0:T(1,128)S(1)} %get-tuple-element.74), channel_id=1, source_target_pairs={{4,0},{8,4},{12,8},{16,12},{20,16},{24,20},{28,24},{0,28},{5,1},{9... | collective-permute-start | bytes 46088 | tf_op jit(solution)/shard_map/ppermute | solution.py:19
  35.7 12.4 %collective-permute-start.3 = (f32[10,70,1]{1,2,0:T(1,128)S(1)}, f32[10,70,1]{1,2,0:T(1,128)S(1)}, u32[]{:S(2)}, u32[]{:S(2)}) collective-permute-start(f32[10,70,1]{1,2,0:T(1,128)S(1)} %copy.174), channel_id=1, source_target_pairs={{1,0},{2,1},{3,2},{5,4},{6,5},{7,6},{9,8},{10,9},{11,10},{13,12},{... | collective-permute-start | bytes 8408 | tf_op jit(solution)/shard_map/ppermute | solution.py:19
  44.8 7.7 %collective-permute-start.2 = (f32[10,70,1]{2,1,0:T(8,128)S(1)}, f32[10,70,1]{2,1,0:T(8,128)}, u32[]{:S(2)}, u32[]{:S(2)}) collective-permute-start(f32[10,70,1]{2,1,0:T(8,128)S(1)} %get-tuple-element.71), channel_id=1, source_target_pairs={{0,1},{1,2},{2,3},{4,5},{5,6},{6,7},{8,9},{9,10},{10,11},{12,13},{... | collective-permute-start | bytes 8408 | tf_op jit(solution)/shard_map/ppermute | solution.py:16
  59.1 1.0 copy-start.1
  59.2 1.0 copy-start.5
  59.2 1.1 copy-start.9
  59.2 1.2 copy-start.13
  60.4 28.9 %collective-permute-start.5 = (f32[8,1,384]{2,0,1:T(8,128)S(1)}, f32[8,1,384]{2,0,1:T(8,128)S(1)}, u32[]{:S(2)}, u32[]{:S(2)}) collective-permute-start(f32[8,1,384]{2,0,1:T(8,128)S(1)} %copy.150), channel_id=1, source_target_pairs={{4,0},{8,4},{12,8},{16,12},{20,16},{24,20},{28,24},{0,28},{5,1},{9... | collective-permute-start | bytes 36872 | tf_op jit(solution)/shard_map/ppermute | solution.py:19
  61.9 26.8 %collective-permute-start.4 = (f32[8,1,384]{2,0,1:T(8,128)S(1)}, f32[8,1,384]{2,0,1:T(8,128)S(1)}, u32[]{:S(2)}, u32[]{:S(2)}) collective-permute-start(f32[8,1,384]{2,0,1:T(8,128)S(1)} %copy.149), channel_id=1, source_target_pairs={{0,4},{4,8},{8,12},{12,16},{16,20},{20,24},{24,28},{28,0},{1,5},{5... | collective-permute-start | bytes 36872 | tf_op jit(solution)/shard_map/ppermute | solution.py:16
  91.8 13.1 %collective-permute-start.6 = (f32[8,70,1]{1,0,2:T(8,128)S(1)}, f32[8,70,1]{1,0,2:T(8,128)S(1)}, u32[]{:S(2)}, u32[]{:S(2)}) collective-permute-start(f32[8,70,1]{1,0,2:T(8,128)S(1)} %get-tuple-element.67), channel_id=1, source_target_pairs={{0,1},{1,2},{2,3},{4,5},{5,6},{6,7},{8,9},{9,10},{10,11},{12,13},{... | collective-permute-start | bytes 6728 | tf_op jit(solution)/shard_map/ppermute | solution.py:16
  102.8 4.9 %collective-permute-start.7 = (f32[8,70,1]{1,0,2:T(8,128)S(1)}, f32[8,70,1]{1,0,2:T(8,128)S(1)}, u32[]{:S(2)}, u32[]{:S(2)}) collective-permute-start(f32[8,70,1]{1,0,2:T(8,128)S(1)} %get-tuple-element.68), channel_id=1, source_target_pairs={{1,0},{2,1},{3,2},{5,4},{6,5},{7,6},{9,8},{10,9},{11,10},{13,12},{... | collective-permute-start | bytes 6728 | tf_op jit(solution)/shard_map/ppermute | solution.py:19
  111.2 2.8 %copy-start.2 = (f32[4,68,384]{2,1,0:T(8,128)S(1)}, f32[4,68,384]{2,1,0:T(8,128)}, u32[]{:S(2)}) copy-start(f32[4,68,384]{2,1,0:T(8,128)} %copy-done.1) | copy-start | bytes 1253380
  111.2 2.8 %copy-start.6 = (f32[4,68,384]{2,1,0:T(8,128)S(1)}, f32[4,68,384]{2,1,0:T(8,128)}, u32[]{:S(2)}) copy-start(f32[4,68,384]{2,1,0:T(8,128)} %copy-done.5) | copy-start | bytes 1253380
  111.2 2.8 %copy-start.10 = (f32[4,68,384]{2,1,0:T(8,128)S(1)}, f32[4,68,384]{2,1,0:T(8,128)}, u32[]{:S(2)}) copy-start(f32[4,68,384]{2,1,0:T(8,128)} %copy-done.9) | copy-start | bytes 1253380
  111.2 2.8 %copy-start.14 = (f32[4,68,384]{2,1,0:T(8,128)S(1)}, f32[4,68,384]{2,1,0:T(8,128)}, u32[]{:S(2)}) copy-start(f32[4,68,384]{2,1,0:T(8,128)} %copy-done.13) | copy-start | bytes 1253380
  115.0 4.3 %copy-start.18 = (f32[2,4,68,384]{3,2,1,0:T(8,128)}, f32[2,4,68,384]{3,2,1,0:T(8,128)S(1)}, u32[]{:S(2)}) copy-start(f32[2,4,68,384]{3,2,1,0:T(8,128)S(1)} %fusion.17) | copy-start | bytes 2506756
  115.0 32.3 %collective-permute-start.8 = (f32[8,1,384]{2,0,1:T(8,128)S(1)}, f32[8,1,384]{2,0,1:T(8,128)S(1)}, u32[]{:S(2)}, u32[]{:S(2)}) collective-permute-start(f32[8,1,384]{2,0,1:T(8,128)S(1)} %copy.157), channel_id=1, source_target_pairs={{0,4},{4,8},{8,12},{12,16},{16,20},{20,24},{24,28},{28,0},{1,5},{5... | collective-permute-start | bytes 36872 | tf_op jit(solution)/shard_map/ppermute | solution.py:16
  116.5 31.4 %collective-permute-start.9 = (f32[8,1,384]{2,0,1:T(8,128)S(1)}, f32[8,1,384]{2,0,1:T(8,128)S(1)}, u32[]{:S(2)}, u32[]{:S(2)}) collective-permute-start(f32[8,1,384]{2,0,1:T(8,128)S(1)} %copy.158), channel_id=1, source_target_pairs={{4,0},{8,4},{12,8},{16,12},{20,16},{24,20},{28,24},{0,28},{5,1},{9... | collective-permute-start | bytes 36872 | tf_op jit(solution)/shard_map/ppermute | solution.py:19
  150.4 10.5 %collective-permute-start.10 = (f32[8,70,1]{1,0,2:T(8,128)S(1)}, f32[8,70,1]{1,0,2:T(8,128)S(1)}, u32[]{:S(2)}, u32[]{:S(2)}) collective-permute-start(f32[8,70,1]{1,0,2:T(8,128)S(1)} %get-tuple-element.65), channel_id=1, source_target_pairs={{0,1},{1,2},{2,3},{4,5},{5,6},{6,7},{8,9},{9,10},{10,11},{12,13},{... | collective-permute-start | bytes 6728 | tf_op jit(solution)/shard_map/ppermute | solution.py:16
  158.8 4.9 %collective-permute-start.11 = (f32[8,70,1]{1,0,2:T(8,128)S(1)}, f32[8,70,1]{1,0,2:T(8,128)S(1)}, u32[]{:S(2)}, u32[]{:S(2)}) collective-permute-start(f32[8,70,1]{1,0,2:T(8,128)S(1)} %get-tuple-element.66), channel_id=1, source_target_pairs={{1,0},{2,1},{3,2},{5,4},{6,5},{7,6},{9,8},{10,9},{11,10},{13,12},{... | collective-permute-start | bytes 6728 | tf_op jit(solution)/shard_map/ppermute | solution.py:19
  167.2 2.8 %copy-start.3 = (f32[4,68,384]{2,1,0:T(8,128)S(1)}, f32[4,68,384]{2,1,0:T(8,128)}, u32[]{:S(2)}) copy-start(f32[4,68,384]{2,1,0:T(8,128)} %copy-done.1) | copy-start | bytes 1253380
  167.2 2.8 %copy-start.7 = (f32[4,68,384]{2,1,0:T(8,128)S(1)}, f32[4,68,384]{2,1,0:T(8,128)}, u32[]{:S(2)}) copy-start(f32[4,68,384]{2,1,0:T(8,128)} %copy-done.5) | copy-start | bytes 1253380
  167.2 2.8 %copy-start.11 = (f32[4,68,384]{2,1,0:T(8,128)S(1)}, f32[4,68,384]{2,1,0:T(8,128)}, u32[]{:S(2)}) copy-start(f32[4,68,384]{2,1,0:T(8,128)} %copy-done.9) | copy-start | bytes 1253380
  167.2 2.8 %copy-start.15 = (f32[4,68,384]{2,1,0:T(8,128)S(1)}, f32[4,68,384]{2,1,0:T(8,128)}, u32[]{:S(2)}) copy-start(f32[4,68,384]{2,1,0:T(8,128)} %copy-done.13) | copy-start | bytes 1253380
  170.0 2.6 %copy-start.22 = (f32[2,4]{1,0:T(2,128)S(1)}, f32[2,4]{1,0:T(2,128)}, u32[]{:S(2)}) copy-start(f32[2,4]{1,0:T(2,128)} %param.25) | copy-start | bytes 100
  170.0 2.6 %copy-start.23 = (f32[2,4]{1,0:T(2,128)S(1)}, f32[2,4]{1,0:T(2,128)}, u32[]{:S(2)}) copy-start(f32[2,4]{1,0:T(2,128)} %param.23) | copy-start | bytes 100
  171.0 1.6 copy-start.17
  171.1 30.1 %collective-permute-start.13 = (f32[8,1,384]{2,0,1:T(8,128)S(1)}, f32[8,1,384]{2,0,1:T(8,128)S(1)}, u32[]{:S(2)}, u32[]{:S(2)}) collective-permute-start(f32[8,1,384]{2,0,1:T(8,128)S(1)} %copy.166), channel_id=1, source_target_pairs={{4,0},{8,4},{12,8},{16,12},{20,16},{24,20},{28,24},{0,28},{5,1},{9... | collective-permute-start | bytes 36872 | tf_op jit(solution)/shard_map/ppermute | solution.py:19
  172.6 28.0 %collective-permute-start.12 = (f32[8,1,384]{2,0,1:T(8,128)S(1)}, f32[8,1,384]{2,0,1:T(8,128)S(1)}, u32[]{:S(2)}, u32[]{:S(2)}) collective-permute-start(f32[8,1,384]{2,0,1:T(8,128)S(1)} %copy.165), channel_id=1, source_target_pairs={{0,4},{4,8},{8,12},{12,16},{16,20},{20,24},{24,28},{28,0},{1,5},{5... | collective-permute-start | bytes 36872 | tf_op jit(solution)/shard_map/ppermute | solution.py:16
  203.6 10.5 %collective-permute-start.14 = (f32[8,70,1]{1,0,2:T(8,128)S(1)}, f32[8,70,1]{1,0,2:T(8,128)S(1)}, u32[]{:S(2)}, u32[]{:S(2)}) collective-permute-start(f32[8,70,1]{1,0,2:T(8,128)S(1)} %get-tuple-element.63), channel_id=1, source_target_pairs={{0,1},{1,2},{2,3},{4,5},{5,6},{6,7},{8,9},{9,10},{10,11},{12,13},{... | collective-permute-start | bytes 6728 | tf_op jit(solution)/shard_map/ppermute | solution.py:16
  212.0 4.9 %collective-permute-start.15 = (f32[8,70,1]{1,0,2:T(8,128)S(1)}, f32[8,70,1]{1,0,2:T(8,128)S(1)}, u32[]{:S(2)}, u32[]{:S(2)}) collective-permute-start(f32[8,70,1]{1,0,2:T(8,128)S(1)} %get-tuple-element.64), channel_id=1, source_target_pairs={{1,0},{2,1},{3,2},{5,4},{6,5},{7,6},{9,8},{10,9},{11,10},{13,12},{... | collective-permute-start | bytes 6728 | tf_op jit(solution)/shard_map/ppermute | solution.py:19
  220.4 2.8 %copy-start.4 = (f32[4,68,384]{2,1,0:T(8,128)S(1)}, f32[4,68,384]{2,1,0:T(8,128)}, u32[]{:S(2)}) copy-start(f32[4,68,384]{2,1,0:T(8,128)} %copy-done.1) | copy-start | bytes 1253380
  220.4 2.8 %copy-start.8 = (f32[4,68,384]{2,1,0:T(8,128)S(1)}, f32[4,68,384]{2,1,0:T(8,128)}, u32[]{:S(2)}) copy-start(f32[4,68,384]{2,1,0:T(8,128)} %copy-done.5) | copy-start | bytes 1253380
  220.4 2.8 %copy-start.12 = (f32[4,68,384]{2,1,0:T(8,128)S(1)}, f32[4,68,384]{2,1,0:T(8,128)}, u32[]{:S(2)}) copy-start(f32[4,68,384]{2,1,0:T(8,128)} %copy-done.9) | copy-start | bytes 1253380
  220.4 2.8 %copy-start.16 = (f32[4,68,384]{2,1,0:T(8,128)S(1)}, f32[4,68,384]{2,1,0:T(8,128)}, u32[]{:S(2)}) copy-start(f32[4,68,384]{2,1,0:T(8,128)} %copy-done.13) | copy-start | bytes 1253380
  223.2 1.0 copy-start.20
  224.4 1.3 copy-start.21
where the time goes:
time: 227 us; the launch traced here: 226 us
  blocking collectives  99.4 us (44%)
  starting transfers between devices  58.3 us (26%)
  local copies, waits for them, and re-layouts  29.4 us (13%)
  other arithmetic  25.4 us (11%)
  waiting for transfers between devices  12.4 us (5%)
    all_gather x4, blocking collectives, local(): every_top = lax.all_gather(top_rows, 'lon', axis=1, tiled=True)  99.4 us
    ppermute x8, starting transfers between devices, extended_2(): lax.ppermute(lax.slice_in_dim(block, block.shape[dim] - width, None, axis...  34.7 us
    ppermute x8, starting transfers between devices, extended_2(): lax.ppermute(lax.slice_in_dim(block, 0, width, axis=dim), axis, backward)  23.7 us
    concatenate x4, other arithmetic, extended_2(): block = jnp.concatenate([low, block, high], axis=dim)  12.1 us
    scatter-add x4, local copies, waits for them, and re-layouts, local(): padded = padded.at[:, :, lat_cells + 1].add(at_top * folded)  9.92 us
    ppermute x8, waiting for transfers between devices, extended_2(): lax.ppermute(lax.slice_in_dim(block, 0, width, axis=dim), axis, backward)  8.54 us
    ppermute x4, local copies, waits for them, and re-layouts, extended_2(): lax.ppermute(lax.slice_in_dim(block, 0, width, axis=dim), axis, backward)  5.23 us
  transfers between devices with their start and end apart: 16, of which 4 were waited for; matrix products, arithmetic and copies ran while one was open for 6% of the time, Pallas kernels for 0%

commit v1 on v0

v1 whole, which is shorter than its diff:
```python
import functools

import jax
import jax.numpy as jnp
from jax import lax
from jax.experimental import pallas as pl
from jax.experimental.pallas import tpu as pltpu
from jax.sharding import PartitionSpec as P

PASSES = 4
LANES = 128
STRAIGHT_ROWS = (1, 2, 3, 2, 1)
MIRROR_ROWS = (2, 3, 4, 3, 2)
MESH = pl.DeviceIdType.MESH


def exchange_kernel(
    n_lon, n_lat,
    f_ref, k_ref, d_ref,
    ew_out, p_out, c_out, q_out,
    ew_buf, p_buf, pt_buf, q_buf, send_sem, recv_sem, local_sem,
):
    stacked, lon_cells, lat_cells = f_ref.shape
    b = lax.axis_index("lon")
    a_lat = lax.axis_index("lat")
    has_n = a_lat < n_lat - 1
    has_s = a_lat > 0
    is_top = a_lat == n_lat - 1
    east = lax.rem(b + 1, n_lon)
    west = lax.rem(b + n_lon - 1, n_lon)
    north = lax.rem(a_lat + 1, n_lat)
    south = lax.rem(a_lat + n_lat - 1, n_lat)

    straight = [
        (slot, STRAIGHT_ROWS[slot], lax.rem(b - (slot - 2) + n_lon, n_lon))
        for slot in (0, 1, 3, 4)
    ]
    mirrored = [
        (5 + slot, MIRROR_ROWS[slot], lax.rem((slot - 2) - b + 2 * n_lon, n_lon))
        for slot in range(5)
    ]

    barrier = pltpu.get_barrier_semaphore()

    def hail(lon, lat):
        pl.semaphore_signal(
            barrier, inc=1, device_id={"lon": lon, "lat": lat}, device_id_type=MESH
        )

    hail(east, a_lat)
    hail(west, a_lat)

    @pl.when(has_n)
    def _():
        for lon in (west, b, east):
            hail(lon, north)

    @pl.when(has_s)
    def _():
        for lon in (west, b, east):
            hail(lon, south)

    @pl.when(is_top)
    def _():
        for _, _, target in straight:
            hail(target, a_lat)
        for _, _, target in mirrored:
            @pl.when(target != b)
            def _():
                hail(target, a_lat)

    expected = 2 + jnp.where(has_n, 3, 0) + jnp.where(has_s, 3, 0) + jnp.where(is_top, 4, 0)
    for _, _, target in mirrored:
        expected = expected + jnp.where(jnp.logical_and(is_top, target != b), 1, 0)

    def read(a, rows, columns):
        if a < stacked:
            return f_ref[a, rows, columns]
        if a == stacked:
            return k_ref[rows, columns]
        return d_ref[rows, columns].astype(jnp.float32)

    arrays = stacked + 2
    everything = slice(0, lat_cells)
    for a in range(arrays):
        half = slice(4 * (a % 2), 4 * (a % 2) + 4)
        ew_buf[0, a // 2, half, :] = read(a, slice(lon_cells - 4, lon_cells), everything)
        ew_buf[1, a // 2, half, :] = read(a, slice(0, 4), everything)

    aligned = (lon_cells // 8) * 8
    for side in range(2):
        p_buf[side, aligned : aligned + 8, :] = jnp.zeros((8, LANES), jnp.float32)
        columns = slice(lat_cells - LANES, lat_cells) if side == 0 else slice(0, LANES)
        for start, count in ((0, aligned), (lon_cells - 8, 8)):
            rows = slice(start, start + count)
            group = lax.broadcasted_iota(jnp.int32, (count, LANES), 1) // 4
            packed = jnp.zeros((count, LANES), jnp.float32)
            for a in range(arrays):
                shift = (4 * a + (4 if side == 0 else 0)) % LANES
                moved = read(a, rows, columns)
                if shift:
                    moved = pltpu.roll(moved, shift, 1)
                packed = jnp.where(group == a, moved, packed)
            p_buf[side, rows, :] = packed

    def remote(src, dst, index, lon, lat):
        return pltpu.make_async_remote_copy(
            src_ref=src, dst_ref=dst, send_sem=send_sem.at[index], recv_sem=recv_sem.at[index],
            device_id={"lon": lon, "lat": lat}, device_id_type=MESH,
        )

    along = [
        remote(ew_buf.at[0], ew_out.at[0], 0, east, a_lat),
        remote(ew_buf.at[1], ew_out.at[1], 1, west, a_lat),
    ]
    tail = pl.ds(aligned, 8)
    head = pl.ds(0, 8)
    up = [
        remote(p_buf.at[0], p_out.at[0], 2, b, north),
        remote(p_buf.at[0, tail], c_out.at[0], 4, east, north),
        remote(p_buf.at[0, head], c_out.at[1], 5, west, north),
    ]
    down = [
        remote(p_buf.at[1], p_out.at[1], 3, b, south),
        remote(p_buf.at[1, tail], c_out.at[2], 6, east, south),
        remote(p_buf.at[1, head], c_out.at[3], 7, west, south),
    ]

    pl.semaphore_wait(barrier, expected)

    for copy in along:
        copy.start()

    @pl.when(has_n)
    def _():
        for copy in up:
            copy.start()

    @pl.when(has_s)
    def _():
        for copy in down:
            copy.start()

    strip_straight = [
        remote(q_buf.at[pl.ds(0, rows + 1)], q_out.at[slot, pl.ds(0, rows + 1)], 8 + slot, target, a_lat)
        for slot, rows, target in straight
    ]
    strip_mirrored = [
        (
            target != b,
            remote(q_buf.at[pl.ds(0, rows + 1)], q_out.at[slot, pl.ds(0, rows + 1)], 8 + slot, target, a_lat),
            pltpu.make_async_copy(
                q_buf.at[pl.ds(0, rows + 1)], q_out.at[slot, pl.ds(0, rows + 1)], local_sem.at[slot]
            ),
        )
        for slot, rows, target in mirrored
    ]
    own = pltpu.make_async_copy(q_buf, q_out.at[2], local_sem.at[2])

    @pl.when(is_top)
    def _():
        square = jnp.concatenate(
            [p_buf[0], jnp.zeros((LANES - p_buf.shape[1], LANES), jnp.float32)], axis=0
        )
        pt_buf[...] = square.T
        q_buf[0] = pt_buf[4 * stacked : 4 * stacked + 8, :]
        for r in range(4):
            q_buf[1 + r] = pt_buf[pl.ds(3 - r, stacked, stride=4), :]
        for copy in strip_straight:
            copy.start()
        for away, copy, stay in strip_mirrored:
            @pl.when(away)
            def _():
                copy.start()

            @pl.when(jnp.logical_not(away))
            def _():
                stay.start()
        own.start()

    for copy in along:
        copy.wait_send()
        copy.wait_recv()

    @pl.when(has_n)
    def _():
        for copy in up:
            copy.wait_send()
        for copy in down:
            copy.wait_recv()

    @pl.when(has_s)
    def _():
        for copy in down:
            copy.wait_send()
        for copy in up:
            copy.wait_recv()

    @pl.when(is_top)
    def _():
        for copy in strip_straight:
            copy.wait_send()
            copy.wait_recv()
        for away, copy, stay in strip_mirrored:
            @pl.when(away)
            def _():
                copy.wait_send()
                copy.wait_recv()

            @pl.when(jnp.logical_not(away))
            def _():
                stay.wait()
        own.wait()


def fold_strip(n_lon, lon_cells, b, q_ref, fp_ref, ghost_ref):
    lane = lax.broadcasted_iota(jnp.int32, (8, LANES), 1)
    sublane = lax.broadcasted_iota(jnp.int32, (8, LANES), 0)
    level = (sublane % 4).astype(jnp.float32)

    def spread(row):
        return jnp.broadcast_to(row, (8, LANES))

    def take(values, index):
        return jnp.take_along_axis(values, index, axis=1, mode="promise_in_bounds")

    kinds = {"S": STRAIGHT_ROWS, "M": MIRROR_ROWS}
    field, kappa, depth, index = {}, {}, {}, {}
    for kind, rows in kinds.items():
        for o in range(-2, 3):
            slot = o + 2 + (0 if kind == "S" else 5)
            block = lax.rem((b if kind == "S" else -b) + o + 2 * n_lon, n_lon)
            index[kind, o] = spread(fp_ref[pl.ds(block, 1), :])
            for r in range(rows[o + 2]):
                kappa[kind, o, r] = spread(q_ref[slot, 0, 3 - r : 4 - r, :])
                depth[kind, o, r] = spread(q_ref[slot, 0, 7 - r : 8 - r, :])
                values = q_ref[slot, 1 + r]
                field[kind, o, r] = jnp.where(depth[kind, o, r] > level, values, 0.0)

    other = {"S": "M", "M": "S"}

    def sides(table, kind, o, r):
        here = table[kind, o, r]
        from_east = table.get((kind, o + 1, r), here)
        from_west = table.get((kind, o - 1, r), here)
        towards = jnp.where(
            lane == lon_cells - 1, pltpu.roll(from_east, lon_cells - 1, 1), pltpu.roll(here, LANES - 1, 1)
        )
        back = jnp.where(
            lane == 0, pltpu.roll(from_west, LANES - lon_cells + 1, 1), pltpu.roll(here, 1, 1)
        )
        return towards, back

    def above(table, kind, o, r):
        if r:
            return table[kind, o, r - 1]
        return take(table[other[kind], -o, 0], index[kind, o])

    faces = {}
    ghosts = []

    def ghost_row(table):
        own = take(table["M", 0, 0], index["S", 0])
        right = take(table["M", -1, 0], index["S", 1])
        left = take(table["M", 1, 0], index["S", -1])
        result = jnp.where(
            lane < 16,
            pltpu.roll(left, (16 - lon_cells) % LANES, 1),
            jnp.where(
                lane < 16 + lon_cells, pltpu.roll(own, 16, 1), pltpu.roll(right, 16 + lon_cells, 1)
            ),
        )
        return jnp.where(jnp.logical_and(lane >= 12, lane < 20 + lon_cells), result, 0.0)

    ghost_kappa = ghost_row(kappa)
    ghost_depth = ghost_row(depth)
    ghosts.append(ghost_row(field))
    for step in range(1, PASSES):
        renewed = {}
        for kind, rows in kinds.items():
            for o in range(-2, 3):
                for r in range(rows[o + 2] - step):
                    if (kind, o, r) not in faces:
                        ke, kw = sides(kappa, kind, o, r)
                        de, dw = sides(depth, kind, o, r)
                        kn, dn = above(kappa, kind, o, r), above(depth, kind, o, r)
                        ks, ds = kappa[kind, o, r + 1], depth[kind, o, r + 1]
                        k0, d0 = kappa[kind, o, r], depth[kind, o, r]
                        faces[kind, o, r] = [
                            jnp.where(jnp.minimum(d0, d) > level, k0 * k, 0.0)
                            for k, d in ((ke, de), (kw, dw), (kn, dn), (ks, ds))
                        ]
                    fe, fw, fn, fs = faces[kind, o, r]
                    x = field[kind, o, r]
                    xe, xw = sides(field, kind, o, r)
                    xn = above(field, kind, o, r)
                    xs = field[kind, o, r + 1]
                    renewed[kind, o, r] = (
                        x + fe * (xe - x) + fw * (xw - x) + fn * (xn - x) + fs * (xs - x)
                    )
        field.update(renewed)
        ghosts.append(ghost_row(field))
    meta = jnp.where(sublane == 0, ghost_kappa, ghost_depth)
    stack = jnp.concatenate(
        ghosts + [meta, jnp.zeros((LANES - 8 * (PASSES + 1), LANES), jnp.float32)], axis=0
    )
    ghost_ref[...] = stack.T


def compute_kernel(
    n_lon, n_lat,
    f_ref, elev_ref, k_ref, d_ref, ratio_ref, fp_ref, sigma_ref, expand_ref,
    ew_ref, p_ref, c_ref, q_ref,
    state_ref, height_ref,
    xa, xb, kx, dx, faces, px, ghost_ref,
):
    stacked, lon_cells, lat_cells = f_ref.shape
    levels = stacked // 2
    b = lax.axis_index("lon")
    a_lat = lax.axis_index("lat")
    is_top = a_lat == n_lat - 1
    is_bottom = a_lat == 0
    rows_total = xa.shape[1]
    tiles = rows_total // 8
    wide = xa.shape[2]
    end = 16 + lon_cells

    @pl.when(is_top)
    def _():
        fold_strip(n_lon, lon_cells, b, q_ref, fp_ref, ghost_ref)

    zero_tile = jnp.zeros((8, wide), jnp.float32)
    for ref in (xa, xb):
        for f in range(stacked):
            ref[f, 0:8, :] = zero_tile
            ref[f, rows_total - 8 : rows_total, :] = zero_tile
    for ref in (kx, dx):
        ref[0:16, :] = jnp.zeros((16, wide), jnp.float32)
        ref[rows_total - 8 : rows_total, :] = zero_tile
    for f in range(stacked):
        xa[f, 8:16, :] = zero_tile
    px[...] = jnp.zeros(px.shape, jnp.float32)

    @pl.when(jnp.logical_not(is_bottom))
    def _():
        px[0, 16:end, :] = p_ref[0, 0:lon_cells, :]
        px[0, 12:16, :] = c_ref[0, lon_cells % 8 - 4 : lon_cells % 8, :]
        px[0, end : end + 4, :] = c_ref[1, 0:4, :]

    @pl.when(jnp.logical_not(is_top))
    def _():
        px[1, 16:end, :] = p_ref[1, 0:lon_cells, :]
        px[1, 12:16, :] = c_ref[2, lon_cells % 8 - 4 : lon_cells % 8, :]
        px[1, end : end + 4, :] = c_ref[3, 0:4, :]

    lane = lax.broadcasted_iota(jnp.int32, (rows_total, LANES), 1)

    def place(ref, own, a):
        ref[16:end, 0:lat_cells] = own
        half = slice(4 * (a % 2), 4 * (a % 2) + 4)
        ref[12:16, 0:lat_cells] = ew_ref[0, a // 2, half, :]
        ref[end : end + 4, 0:lat_cells] = ew_ref[1, a // 2, half, :]
        below = pltpu.roll(px[0], LANES - 4 - 4 * a, 1)
        up = px[1]
        if a:
            up = pltpu.roll(up, LANES - 4 * a, 1)
        ref[:, lat_cells:wide] = jnp.where(lane < 4, up, jnp.where(lane >= LANES - 4, below, 0.0))

    for f in range(stacked):
        place(xa.at[f], f_ref[f], f)
    place(kx, k_ref[...], stacked)
    place(dx, d_ref[...].astype(jnp.float32), stacked + 1)

    def refresh(ref, which):
        moved = ghost_ref[0:rows_total, :]
        if which:
            moved = pltpu.roll(moved, LANES - which, 1)
        ref[:, lat_cells:wide] = jnp.where(lane == 0, moved, ref[:, lat_cells:wide])

    @pl.when(is_top)
    def _():
        refresh(kx, 8 * PASSES)
        refresh(dx, 8 * PASSES + 1)

    for i in range(1, tiles - 1):
        at = slice(8 * i, 8 * i + 8)
        k0, d0 = kx[at, :], dx[at, :]
        pairs = []
        for rows in (slice(8 * i + 1, 8 * i + 9), slice(8 * i - 1, 8 * i + 7)):
            pairs.append((kx[rows, :], dx[rows, :]))
        for shift in (wide - 1, 1):
            pairs.append((pltpu.roll(k0, shift, 1), pltpu.roll(d0, shift, 1)))
        pairs = [(k0 * k, jnp.minimum(d0, d)) for k, d in pairs]
        for level in range(levels):
            total = jnp.ones((8, wide), jnp.float32)
            for side, (product, least) in enumerate(pairs):
                face = jnp.where(least > float(level), product, 0.0)
                faces[level, side, at, :] = face
                total = total - face
            faces[level, 4, at, :] = total
            for c in range(2):
                f = c * levels + level
                xa[f, at, :] = jnp.where(d0 > float(level), xa[f, at, :], 0.0)

    source, target = xa, xb
    for step in range(PASSES):
        @pl.when(is_top)
        def _(source=source, step=step):
            for f in range(stacked):
                refresh(source.at[f], 8 * step + f)

        def one_level(level, carry, source=source, target=target):
            for i in range(1, tiles - 1):
                at = slice(8 * i, 8 * i + 8)
                fe, fw, fn, fs, fc = [faces[level, side, at, :] for side in range(5)]
                for c in range(2):
                    f = c * levels + level
                    x = source[f, at, :]
                    xe = source[f, 8 * i + 1 : 8 * i + 9, :]
                    xw = source[f, 8 * i - 1 : 8 * i + 7, :]
                    xn = pltpu.roll(x, wide - 1, 1)
                    xs = pltpu.roll(x, 1, 1)
                    target[f, at, :] = fc * x + fe * xe + fw * xw + fn * xn + fs * xs
            return carry

        lax.fori_loop(0, levels, one_level, 0)
        source, target = target, source

    for start in range(0, lon_cells, 8):
        count = min(8, lon_cells - start)
        out = slice(start, start + count)
        at = slice(16 + start, 16 + start + count)
        ratio = ratio_ref[out, :]
        height = elev_ref[out, :]
        for level in range(levels):
            thermal = sigma_ref[0, level] * source[level, at, 0:lat_cells]
            salt = sigma_ref[1, level] * source[levels + level, at, 0:lat_cells] + ratio * thermal
            state_ref[level, out, :] = thermal
            state_ref[levels + level, out, :] = salt
            height = height + (expand_ref[0, level] * thermal + expand_ref[1, level] * salt)
        height_ref[out, :] = height


def local(
    n_lon, n_lat,
    control_fields,
    unexplained_elevation,
    diffusivity,
    depth_levels,
    fold_partner,
    prior_sigmas,
    haline_thermal_ratio,
    expansion_coefficients,
):
    levels, lon_cells, lat_cells = control_fields.shape[1:]
    stacked = 2 * levels
    fields = control_fields.reshape(stacked, lon_cells, lat_cells)
    partners = jnp.pad(
        (fold_partner % lon_cells).reshape(n_lon, lon_cells), ((0, 0), (0, LANES - lon_cells))
    )
    pairs = (stacked + 2) // 2
    tall = -(-lon_cells // 8) * 8
    f32 = jnp.float32
    vmem = pl.BlockSpec(memory_space=pltpu.VMEM)
    smem = pl.BlockSpec(memory_space=pltpu.SMEM)
    anywhere = pl.BlockSpec(memory_space=pl.ANY)
    halos = pl.pallas_call(
        functools.partial(exchange_kernel, n_lon, n_lat),
        name="exchange",
        out_shape=(
            jax.ShapeDtypeStruct((2, pairs, 8, lat_cells), f32),
            jax.ShapeDtypeStruct((2, tall, LANES), f32),
            jax.ShapeDtypeStruct((4, 8, LANES), f32),
            jax.ShapeDtypeStruct((10, 5, 8, LANES), f32),
        ),
        in_specs=[vmem] * 3,
        out_specs=(anywhere,) * 4,
        scratch_shapes=[
            pltpu.VMEM((2, pairs, 8, lat_cells), f32),
            pltpu.VMEM((2, tall, LANES), f32),
            pltpu.VMEM((LANES, LANES), f32),
            pltpu.VMEM((5, 8, LANES), f32),
            pltpu.SemaphoreType.DMA((18,)),
            pltpu.SemaphoreType.DMA((18,)),
            pltpu.SemaphoreType.DMA((10,)),
        ],
        compiler_params=pltpu.CompilerParams(collective_id=0, has_side_effects=True),
    )(fields, diffusivity, depth_levels)
    wide = lat_cells + LANES
    tiles = 16 + tall + 8
    state, height = pl.pallas_call(
        functools.partial(compute_kernel, n_lon, n_lat),
        name="diffuse",
        out_shape=(
            jax.ShapeDtypeStruct((stacked, lon_cells, lat_cells), f32),
            jax.ShapeDtypeStruct((lon_cells, lat_cells), f32),
        ),
        in_specs=[vmem] * 6 + [smem] * 2 + [vmem] * 4,
        out_specs=(vmem, vmem),
        scratch_shapes=[
            pltpu.VMEM((stacked, tiles, wide), f32),
            pltpu.VMEM((stacked, tiles, wide), f32),
            pltpu.VMEM((tiles, wide), f32),
            pltpu.VMEM((tiles, wide), f32),
            pltpu.VMEM((levels, 5, tiles, wide), f32),
            pltpu.VMEM((2, tiles, LANES), f32),
            pltpu.VMEM((LANES, LANES), f32),
        ],
        compiler_params=pltpu.CompilerParams(vmem_limit_bytes=40 * 1024 * 1024),
    )(
        fields, unexplained_elevation, diffusivity, depth_levels, haline_thermal_ratio,
        partners, prior_sigmas, expansion_coefficients, *halos,
    )
    return state.reshape(2, levels, lon_cells, lat_cells), height


def solution(mesh):
    return jax.shard_map(
        functools.partial(local, mesh.shape["lon"], mesh.shape["lat"]),
        mesh=mesh,
        in_specs=(
            P(None, None, "lon", "lat"),
            P("lon", "lat"),
            P("lon", "lat"),
            P("lon", "lat"),
            P(),
            P(),
            P("lon", "lat"),
            P(),
        ),
        out_specs=(P(None, None, "lon", "lat"), P("lon", "lat")),
        check_vma=False,
    )
```

time: 227 us -> 27.1 us (0.12)
  blocking collectives: 99.4 us -> 0 us
  starting transfers between devices: 58.3 us -> 0 us
  other arithmetic: 25.4 us -> 0.7 us
  local copies, waits for them, and re-layouts: 29.4 us -> 7.44 us
  Pallas kernels: 0 us -> 17.9 us
  waiting for transfers between devices: 12.4 us -> 0 us
    all_gather x4 -> x0, blocking collectives: 99.4 us -> none  [local(): every_top = lax.all_gather(top_rows, 'lon', axis=1, tiled=True)]
    ppermute x16 -> x0, starting transfers between devices: 58.3 us -> none  [the longest x8 34.7 us: extended_2(): lax.ppermute(lax.slice_in_dim(block, block.shape[dim] - width, None, axis...]
    pallas_call x0 -> x2, Pallas kernels: none -> 17.9 us  [the longest x1 11.7 us: local(): pl.pallas_call(functools.partial(exchange_kernel, n_lon, n_lat), name='ex...]
    concatenate x9 -> x0, other arithmetic: 12.6 us -> none  [the longest x4 12.1 us: extended_2(): block = jnp.concatenate([low, block, high], axis=dim)]
    ppermute x16 -> x0, waiting for transfers between devices: 12.4 us -> none  [the longest x8 8.54 us: extended_2(): lax.ppermute(lax.slice_in_dim(block, 0, width, axis=dim), axis, backward)]
    scatter-add x4 -> x0, local copies, waits for them, and re-layouts: 9.92 us -> none  [local(): padded = padded.at[:, :, lat_cells + 1].add(at_top * folded)]
    ppermute x7 -> x0, local copies, waits for them, and re-layouts: 7.04 us -> none  [the longest x4 5.23 us: extended_2(): lax.ppermute(lax.slice_in_dim(block, 0, width, axis=dim), axis, backward)]
    unnamed x51 -> x24, local copies, waits for them, and re-layouts: 2.06 us -> 7.36 us
  transfers between devices with their start and end apart: 16 -> 0, of which waited for: 4 -> 0; matrix products, arithmetic and copies ran while one was open for 6% -> 0% of each run, Pallas kernels for 0% -> 0%
where the time goes in v1:
time: 27.1 us; the launch traced here: 26.7 us
  Pallas kernels  17.9 us (66%)
  local copies, waits for them, and re-layouts  7.44 us (27%)
  between operations  0.72 us (3%)
  other arithmetic  0.7 us (3%)
    pallas_call x1, Pallas kernels, local(): pl.pallas_call(functools.partial(exchange_kernel, n_lon, n_lat), name='ex...  11.7 us
    unnamed x24, local copies, waits for them, and re-layouts  7.36 us
    pallas_call x1, Pallas kernels, local(): pl.pallas_call(functools.partial(compute_kernel, n_lon, n_lat), name='dif...  6.19 us
    select_n x1, other arithmetic, local(): fold_partner % lon_cells  0.7 us

profile of v1, /device:TPU:1, one launch (start us, length us, event | category | flops | bytes accessed | tf_op | source)
XLA Modules:
  0.0 26.7 jit_solution(17063242129463013490)
XLA Ops:
  0.6 0.7 %add_select_fusion = s32[544]{0:T(1024)S(1)} fusion(s32[544]{0:T(1024)} %param.12), kind=kLoop, calls=%fused_computation | loop fusion | flops 3264 | bytes 4352 | tf_op jit(solution)/shard_map/jit(remainder)/select_n | solution.py:459
  1.3 0.1 reshape.14
  1.4 0.0 copy-start.5
  1.4 0.0 copy-start.6
  1.4 2.2 %copy.10 = f32[2,4,68,384]{3,2,1,0:T(8,128)} copy(f32[2,4,68,384]{3,1,2,0:T(4,128)} %param.8) | data formatting | bytes 1671168 | tf_op args[0]
  3.6 0.0 copy-start
  3.6 0.0 copy-start.1
  3.6 0.0 copy-start.2
  3.6 0.0 copy-start.10
  3.6 11.7 %exchange.1 = (f32[2,5,8,384]{3,2,1,0:T(8,128)}, f32[2,72,128]{2,1,0:T(8,128)}, f32[4,8,128]{2,1,0:T(8,128)}, f32[10,5,8,128]{3,2,1,0:T(8,128)}) custom-call(f32[8,68,384]{2,1,0:T(8,128)} %bitcast.2, f32[68,384]{1,0:T(8,128)} %k_ref.3, s32[68,384]{1,0:T(8,128)} %d_ref.3), custom_call_target="tpu_custom_call" | custom-call | tf_op jit(solution)/shard_map/exchange/pallas_call | solution.py:467
  15.3 0.0 copy-start.9
  15.3 0.0 copy-done.5
  15.3 0.0 copy-done.6
  15.4 0.0 copy-done
  15.4 0.0 copy-done.1
  15.4 0.0 copy-done.2
  15.4 0.0 copy-done.10
  15.4 0.6 %copy-done.9 = f32[2,4]{1,0:T(2,128)S(1)} copy-done((f32[2,4]{1,0:T(2,128)S(1)}, f32[2,4]{1,0:T(2,128)}, u32[]{:S(2)}) %copy-start.9) | copy-done | bytes 56
  16.0 0.0 copy-start.3
  16.0 0.9 %copy-done.3 = f32[10,5,8,128]{3,2,1,0:T(8,128)S(1)} copy-done((f32[10,5,8,128]{3,2,1,0:T(8,128)S(1)}, f32[10,5,8,128]{3,2,1,0:T(8,128)}, u32[]{:S(2)}) %copy-start.3) | copy-done | bytes 204824
  16.9 0.0 copy-start.4
  16.9 0.9 %copy-done.4 = f32[2,5,8,384]{3,2,1,0:T(8,128)S(1)} copy-done((f32[2,5,8,384]{3,2,1,0:T(8,128)S(1)}, f32[2,5,8,384]{3,2,1,0:T(8,128)}, u32[]{:S(2)}) %copy-start.4) | copy-done | bytes 122904
  17.8 0.0 copy-start.7
  17.8 0.9 %copy-done.7 = f32[2,72,128]{2,1,0:T(8,128)S(1)} copy-done((f32[2,72,128]{2,1,0:T(8,128)S(1)}, f32[2,72,128]{2,1,0:T(8,128)}, u32[]{:S(2)}) %copy-start.7) | copy-done | bytes 73752
  18.7 0.0 copy-start.8
  18.7 0.7 %copy-done.8 = f32[4,8,128]{2,1,0:T(8,128)S(1)} copy-done((f32[4,8,128]{2,1,0:T(8,128)S(1)}, f32[4,8,128]{2,1,0:T(8,128)}, u32[]{:S(2)}) %copy-start.8) | copy-done | bytes 16408
  19.4 6.2 %diffuse.1 = (f32[8,68,384]{2,1,0:T(8,128)S(1)}, f32[68,384]{1,0:T(8,128)}) custom-call(f32[8,68,384]{2,1,0:T(8,128)S(1)} %bitcast.3, f32[68,384]{1,0:T(8,128)S(1)} %copy-done.5, f32[68,384]{1,0:T(8,128)S(1)} %copy-done.1, s32[68,384]{1,0:T(8,128)S(1)} %copy-done.2, f32[68,384]{1,0:T(8,128)S(1)} %copy-done.6, s32[8,128]{1,0:T(8,128)S(1)} %pad.4.fp_ref, ...), custom_call_target="tpu_custom_call" | custom-call | tf_op jit(solution)/shard_map/diffuse/pallas_call | solution.py:491
  25.6 1.1 %copy.11 = f32[2,4,68,384]{3,1,2,0:T(4,128)} copy(f32[2,4,68,384]{3,2,1,0:T(8,128)S(1)} %bitcast.4) | data formatting | bytes 1671168
  (1 shorter events, 0.0 us)
Async XLA Ops:
  1.4 13.9 %copy-start.5 = (f32[68,384]{1,0:T(8,128)S(1)}, f32[68,384]{1,0:T(8,128)}, u32[]{:S(2)}) copy-start(f32[68,384]{1,0:T(8,128)} %elev_ref.1) | copy-start | bytes 313348
  1.4 13.9 %copy-start.6 = (f32[68,384]{1,0:T(8,128)S(1)}, f32[68,384]{1,0:T(8,128)}, u32[]{:S(2)}) copy-start(f32[68,384]{1,0:T(8,128)} %ratio_ref.1) | copy-start | bytes 313348
  3.6 11.7 %copy-start = (f32[2,4,68,384]{3,2,1,0:T(8,128)S(1)}, f32[2,4,68,384]{3,2,1,0:T(8,128)}, u32[]{:S(2)}) copy-start(f32[2,4,68,384]{3,2,1,0:T(8,128)} %copy.10) | copy-start | bytes 2506756
  3.6 11.7 %copy-start.1 = (f32[68,384]{1,0:T(8,128)S(1)}, f32[68,384]{1,0:T(8,128)}, u32[]{:S(2)}) copy-start(f32[68,384]{1,0:T(8,128)} %k_ref.3) | copy-start | bytes 313348
  3.6 11.8 %copy-start.2 = (s32[68,384]{1,0:T(8,128)S(1)}, s32[68,384]{1,0:T(8,128)}, u32[]{:S(2)}) copy-start(s32[68,384]{1,0:T(8,128)} %d_ref.3) | copy-start | bytes 313348
  3.6 11.8 %copy-start.10 = (f32[2,4]{1,0:T(2,128)S(1)}, f32[2,4]{1,0:T(2,128)}, u32[]{:S(2)}) copy-start(f32[2,4]{1,0:T(2,128)} %expand_ref.1) | copy-start | bytes 100
  15.3 0.7 %copy-start.9 = (f32[2,4]{1,0:T(2,128)S(1)}, f32[2,4]{1,0:T(2,128)}, u32[]{:S(2)}) copy-start(f32[2,4]{1,0:T(2,128)} %sigma_ref.1) | copy-start | bytes 100
  16.0 0.9 %copy-start.3 = (f32[10,5,8,128]{3,2,1,0:T(8,128)S(1)}, f32[10,5,8,128]{3,2,1,0:T(8,128)}, u32[]{:S(2)}) copy-start(f32[10,5,8,128]{3,2,1,0:T(8,128)} %get-tuple-element.11.q_ref) | copy-start | bytes 614404
  16.9 0.9 %copy-start.4 = (f32[2,5,8,384]{3,2,1,0:T(8,128)S(1)}, f32[2,5,8,384]{3,2,1,0:T(8,128)}, u32[]{:S(2)}) copy-start(f32[2,5,8,384]{3,2,1,0:T(8,128)} %get-tuple-element.8.ew_ref) | copy-start | bytes 368644
  17.8 0.9 %copy-start.7 = (f32[2,72,128]{2,1,0:T(8,128)S(1)}, f32[2,72,128]{2,1,0:T(8,128)}, u32[]{:S(2)}) copy-start(f32[2,72,128]{2,1,0:T(8,128)} %get-tuple-element.9.p_ref) | copy-start | bytes 221188
  18.7 0.7 %copy-start.8 = (f32[4,8,128]{2,1,0:T(8,128)S(1)}, f32[4,8,128]{2,1,0:T(8,128)}, u32[]{:S(2)}) copy-start(f32[4,8,128]{2,1,0:T(8,128)} %get-tuple-element.10.c_ref) | copy-start | bytes 49156

commit v2 on v1

v2 whole, which is shorter than its diff:
```python
import functools

import jax
import jax.numpy as jnp
from jax import lax
from jax.experimental import pallas as pl
from jax.experimental.pallas import tpu as pltpu
from jax.sharding import PartitionSpec as P

PASSES = 4
LANES = 128
STRAIGHT_ROWS = (1, 2, 3, 2, 1)
MIRROR_ROWS = (2, 3, 4, 3, 2)
PLACES = (1, 0, 3)
MESH = pl.DeviceIdType.MESH


def exchange_kernel(
    n_lon, n_lat,
    f_ref, k_ref, d_ref,
    ew_out, kd_out, p_out, c_out, q_out,
    edge_buf, tail_buf, kd_buf, p_buf, send_sem, recv_sem, local_sem, load_sem,
):
    lon_cells, lat_cells = k_ref.shape
    b = lax.axis_index("lon")
    a_lat = lax.axis_index("lat")
    has_n = a_lat < n_lat - 1
    has_s = a_lat > 0
    is_top = a_lat == n_lat - 1
    east = lax.rem(b + 1, n_lon)
    west = lax.rem(b + n_lon - 1, n_lon)
    north = lax.rem(a_lat + 1, n_lat)
    south = lax.rem(a_lat + n_lat - 1, n_lat)

    loads = [
        pltpu.make_async_copy(
            f_ref.at[c, :, :, pl.ds(start, LANES)],
            edge_buf.at[side, :, pl.ds(4 * c, 4), :],
            load_sem.at[2 * side + c],
        )
        for side, start in ((0, lat_cells - LANES), (1, 0))
        for c in range(2)
    ]
    for copy in loads:
        copy.start()

    straight = [
        (slot, lax.rem(b - (slot - 2) + n_lon, n_lon))
        for slot in (0, 1, 3, 4)
    ]
    mirrored = [
        (5 + slot, lax.rem((slot - 2) - b + 2 * n_lon, n_lon))
        for slot in range(5)
    ]

    barrier = pltpu.get_barrier_semaphore()

    def hail(lon, lat):
        pl.semaphore_signal(
            barrier, inc=1, device_id={"lon": lon, "lat": lat}, device_id_type=MESH
        )

    hail(east, a_lat)
    hail(west, a_lat)

    @pl.when(has_n)
    def _():
        for lon in (west, b, east):
            hail(lon, north)

    @pl.when(has_s)
    def _():
        for lon in (west, b, east):
            hail(lon, south)

    @pl.when(is_top)
    def _():
        for _, target in straight:
            hail(target, a_lat)
        for _, target in mirrored:
            @pl.when(target != b)
            def _():
                hail(target, a_lat)

    expected = 2 + jnp.where(has_n, 3, 0) + jnp.where(has_s, 3, 0) + jnp.where(is_top, 4, 0)
    for _, target in mirrored:
        expected = expected + jnp.where(jnp.logical_and(is_top, target != b), 1, 0)

    def remote(src, dst, index, lon, lat):
        return pltpu.make_async_remote_copy(
            src_ref=src, dst_ref=dst, send_sem=send_sem.at[index], recv_sem=recv_sem.at[index],
            device_id={"lon": lon, "lat": lat}, device_id_type=MESH,
        )

    last = pl.ds(lon_cells - 4, 4)
    first = pl.ds(0, 4)
    far = [
        remote(f_ref.at[:, last], ew_out.at[0], 0, east, a_lat),
        remote(f_ref.at[:, first], ew_out.at[1], 1, west, a_lat),
    ]
    pl.semaphore_wait(barrier, expected)
    for copy in far:
        copy.start()

    for source, start in ((k_ref, 0), (d_ref, 4)):
        kd_buf[0, start : start + 4, :] = source[lon_cells - 4 : lon_cells, :].astype(jnp.float32)
        kd_buf[1, start : start + 4, :] = source[0:4, :].astype(jnp.float32)

    lane = lax.broadcasted_iota(jnp.int32, (8, LANES), 1)
    aligned = (lon_cells // 8) * 8
    for side in range(2):
        columns = slice(lat_cells - LANES, lat_cells) if side == 0 else slice(0, LANES)
        offset = 4 if side == 0 else 0
        packed = jnp.zeros((8, LANES), jnp.float32)
        for which, source in enumerate((k_ref, d_ref)):
            tail_buf[...] = jnp.zeros((8, LANES), jnp.float32)
            tail_buf[0 : lon_cells - aligned, :] = source[aligned:lon_cells, columns].astype(jnp.float32)
            for j in range(-(-lon_cells // 8)):
                if 8 * j < aligned:
                    moved = source[8 * j : 8 * j + 8, columns].astype(jnp.float32)
                else:
                    moved = tail_buf[...]
                shift = (8 * j + 4 * which + offset) % LANES
                if shift:
                    moved = pltpu.roll(moved, shift, 1)
                packed = jnp.where(lane // 4 == 2 * j + which, moved, packed)
        p_buf[side, :, 2 * LANES : 3 * LANES] = packed

    for copy in loads:
        copy.wait()
    for side in range(2):
        offset = 4 if side == 0 else 0
        for group in range(3):
            packed = jnp.zeros((8, LANES), jnp.float32)
            for col in range(32 * group, min(32 * group + 32, lon_cells)):
                shift = (4 * (col % 32) + offset) % LANES
                moved = edge_buf[side, col]
                if shift:
                    moved = pltpu.roll(moved, shift, 1)
                packed = jnp.where(lane // 4 == col % 32, moved, packed)
            place = PLACES[group] * LANES
            p_buf[side, :, place : place + LANES] = packed

    along = [
        remote(kd_buf.at[0], kd_out.at[0], 18, east, a_lat),
        remote(kd_buf.at[1], kd_out.at[1], 19, west, a_lat),
    ]
    tail = pl.ds(2 * LANES, 2 * LANES)
    head = pl.ds(LANES, 2 * LANES)
    up = [
        remote(p_buf.at[0], p_out.at[0], 2, b, north),
        remote(p_buf.at[0, :, tail], c_out.at[0], 4, east, north),
        remote(p_buf.at[0, :, head], c_out.at[1], 5, west, north),
    ]
    down = [
        remote(p_buf.at[1], p_out.at[1], 3, b, south),
        remote(p_buf.at[1, :, tail], c_out.at[2], 6, east, south),
        remote(p_buf.at[1, :, head], c_out.at[3], 7, west, south),
    ]

    for copy in along:
        copy.start()

    @pl.when(has_n)
    def _():
        for copy in up:
            copy.start()

    @pl.when(has_s)
    def _():
        for copy in down:
            copy.start()

    strip_straight = [
        remote(p_buf.at[0], q_out.at[slot], 8 + slot, target, a_lat) for slot, target in straight
    ]
    strip_mirrored = [
        (
            target != b,
            remote(p_buf.at[0], q_out.at[slot], 8 + slot, target, a_lat),
            pltpu.make_async_copy(p_buf.at[0], q_out.at[slot], local_sem.at[slot]),
        )
        for slot, target in mirrored
    ]
    own = pltpu.make_async_copy(p_buf.at[0], q_out.at[2], local_sem.at[2])

    @pl.when(is_top)
    def _():
        for copy in strip_straight:
            copy.start()
        for away, copy, stay in strip_mirrored:
            @pl.when(away)
            def _():
                copy.start()

            @pl.when(jnp.logical_not(away))
            def _():
                stay.start()
        own.start()

    for copy in far + along:
        copy.wait_send()
        copy.wait_recv()

    @pl.when(has_n)
    def _():
        for copy in up:
            copy.wait_send()
        for copy in down:
            copy.wait_recv()

    @pl.when(has_s)
    def _():
        for copy in down:
            copy.wait_send()
        for copy in up:
            copy.wait_recv()

    @pl.when(is_top)
    def _():
        for copy in strip_straight:
            copy.wait_send()
            copy.wait_recv()
        for away, copy, stay in strip_mirrored:
            @pl.when(away)
            def _():
                copy.wait_send()
                copy.wait_recv()

            @pl.when(jnp.logical_not(away))
            def _():
                stay.wait()
        own.wait()


def fold_strip(n_lon, lon_cells, b, q_ref, fp_ref, ghost_ref, coast_ref):
    lane = lax.broadcasted_iota(jnp.int32, (8, LANES), 1)
    sublane = lax.broadcasted_iota(jnp.int32, (8, LANES), 0)
    level = (sublane % 4).astype(jnp.float32)

    def spread(row):
        return jnp.broadcast_to(row, (8, LANES))

    def take(values, index):
        return jnp.take_along_axis(values, index, axis=1, mode="promise_in_bounds")

    kinds = {"S": STRAIGHT_ROWS, "M": MIRROR_ROWS}
    field, kappa, depth, index = {}, {}, {}, {}

    def tile(slot, place):
        return q_ref[slot, :, place * LANES : (place + 1) * LANES]

    def column_of(values, start):
        picked = take(values, 8 * (lane // 8) + start)
        return spread(jnp.sum(jnp.where(sublane == lane % 8, picked, 0.0), axis=0, keepdims=True))

    for kind, rows in kinds.items():
        for o in range(-2, 3):
            slot = o + 2 + (0 if kind == "S" else 5)
            block = lax.rem((b if kind == "S" else -b) + o + 2 * n_lon, n_lon)
            opposite = lax.rem(n_lon - block, n_lon)
            index[kind, o] = jnp.maximum(
                spread(fp_ref[pl.ds(block, 1), :]) - opposite * lon_cells, 0
            )
            parts = [tile(slot, place) for place in PLACES]
            meta = tile(slot, 2)
            for r in range(rows[o + 2]):
                kappa[kind, o, r] = column_of(meta, 3 - r)
                depth[kind, o, r] = column_of(meta, 7 - r)
                pieces = [take(part, 4 * (lane % 32) + 3 - r) for part in parts]
                values = jnp.where(
                    lane < 32, pieces[0], jnp.where(lane < 64, pieces[1], pieces[2])
                )
                field[kind, o, r] = jnp.where(depth[kind, o, r] > level, values, 0.0)

    other = {"S": "M", "M": "S"}

    def sides(table, kind, o, r):
        here = table[kind, o, r]
        from_east = table.get((kind, o + 1, r), here)
        from_west = table.get((kind, o - 1, r), here)
        towards = jnp.where(
            lane == lon_cells - 1, pltpu.roll(from_east, lon_cells - 1, 1), pltpu.roll(here, LANES - 1, 1)
        )
        back = jnp.where(
            lane == 0, pltpu.roll(from_west, LANES - lon_cells + 1, 1), pltpu.roll(here, 1, 1)
        )
        return towards, back

    def above(table, kind, o, r):
        if r:
            return table[kind, o, r - 1]
        return take(table[other[kind], -o, 0], index[kind, o])

    faces = {}
    ghosts = []

    def ghost_row(table):
        own = take(table["M", 0, 0], index["S", 0])
        right = take(table["M", -1, 0], index["S", 1])
        left = take(table["M", 1, 0], index["S", -1])
        result = jnp.where(
            lane < 4,
            pltpu.roll(left, (4 - lon_cells) % LANES, 1),
            jnp.where(
                lane < 4 + lon_cells, pltpu.roll(own, 4, 1), pltpu.roll(right, 4 + lon_cells, 1)
            ),
        )
        return jnp.where(lane < 8 + lon_cells, result, 0.0)

    ghost_kappa = ghost_row(kappa)
    ghost_depth = ghost_row(depth)
    ghosts.append(ghost_row(field))
    for step in range(1, PASSES):
        renewed = {}
        for kind, rows in kinds.items():
            for o in range(-2, 3):
                for r in range(rows[o + 2] - step):
                    if (kind, o, r) not in faces:
                        ke, kw = sides(kappa, kind, o, r)
                        de, dw = sides(depth, kind, o, r)
                        kn, dn = above(kappa, kind, o, r), above(depth, kind, o, r)
                        ks, ds = kappa[kind, o, r + 1], depth[kind, o, r + 1]
                        k0, d0 = kappa[kind, o, r], depth[kind, o, r]
                        faces[kind, o, r] = [
                            jnp.where(jnp.minimum(d0, d) > level, k0 * k, 0.0)
                            for k, d in ((ke, de), (kw, dw), (kn, dn), (ks, ds))
                        ]
                    fe, fw, fn, fs = faces[kind, o, r]
                    x = field[kind, o, r]
                    xe, xw = sides(field, kind, o, r)
                    xn = above(field, kind, o, r)
                    xs = field[kind, o, r + 1]
                    renewed[kind, o, r] = (
                        x + fe * (xe - x) + fw * (xw - x) + fn * (xn - x) + fs * (xs - x)
                    )
        field.update(renewed)
        ghosts.append(ghost_row(field))
    for step in range(PASSES):
        ghost_ref[step] = ghosts[step]
    for which, row in ((0, ghost_kappa), (1, ghost_depth)):
        square = jnp.concatenate([row, jnp.zeros((LANES - 8, LANES), jnp.float32)], axis=0).T
        coast_ref[which, 0:4, :] = jnp.zeros((4, LANES), jnp.float32)
        coast_ref[which, 4 : 8 + LANES - 4, :] = square[0:LANES, :]


def compute_kernel(
    n_lon, n_lat,
    f_ref, elev_ref, k_ref, d_ref, ratio_ref, fp_ref, sigma_ref, expand_ref,
    ew_hbm, kd_hbm, p_hbm, c_hbm, q_hbm,
    state_hbm, height_ref,
    xa, xb, ya, kx, dx, lon_k, lon_d, lat_k, lat_d, e_face, n_face,
    kd_ref, p_ref, c_ref, q_ref, ghost_ref, coast_ref, sems, out_sems,
):
    lon_cells, lat_cells = k_ref.shape
    wide = xa.shape[2]
    count = lon_cells + 8
    tall = kx.shape[0]
    b = lax.axis_index("lon")
    a_lat = lax.axis_index("lat")
    is_top = a_lat == n_lat - 1
    is_bottom = a_lat == 0

    small = [
        pltpu.make_async_copy(kd_hbm, kd_ref, sems.at[0]),
        pltpu.make_async_copy(p_hbm, p_ref, sems.at[1]),
        pltpu.make_async_copy(c_hbm, c_ref, sems.at[2]),
        pltpu.make_async_copy(q_hbm, q_ref, sems.at[3]),
    ]
    large = []
    for c in range(2):
        half = pl.ds(4 * c, 4)
        own = pl.ds(0, lat_cells)
        large += [
            pltpu.make_async_copy(ew_hbm.at[0, c], xa.at[pl.ds(0, 4), half, own], sems.at[4 + c]),
            pltpu.make_async_copy(
                ew_hbm.at[1, c], xa.at[pl.ds(lon_cells + 4, 4), half, own], sems.at[6 + c]
            ),
            pltpu.make_async_copy(f_ref.at[c], xa.at[pl.ds(4, lon_cells), half, own], sems.at[8 + c]),
        ]
    for copy in small + large:
        copy.start()

    sublane = lax.broadcasted_iota(jnp.int32, (8, LANES), 0)
    lane = lax.broadcasted_iota(jnp.int32, (8, LANES), 1)
    for ref, source in ((kx, k_ref), (dx, d_ref)):
        ref[0:8, :] = jnp.zeros((8, wide), jnp.float32)
        ref[8 : 8 + lon_cells, 0:lat_cells] = source[...].astype(jnp.float32)

    for copy in small:
        copy.wait()

    kx[4:8, 0:lat_cells] = kd_ref[0, 0:4, :]
    dx[4:8, 0:lat_cells] = kd_ref[0, 4:8, :]
    kx[8 + lon_cells : 12 + lon_cells, 0:lat_cells] = kd_ref[1, 0:4, :]
    dx[8 + lon_cells : 12 + lon_cells, 0:lat_cells] = kd_ref[1, 4:8, :]

    def part(ref, place):
        return ref[:, place * LANES : (place + 1) * LANES]

    def clean(present, values):
        return jnp.where(present, values, 0.0)

    no_n, no_s = jnp.logical_not(is_top), jnp.logical_not(is_bottom)
    south = [clean(no_s, part(p_ref.at[0], place)) for place in PLACES]
    north = [clean(no_n, part(p_ref.at[1], place)) for place in PLACES]
    south_west = clean(no_s, part(c_ref.at[0], 1))
    south_east = clean(no_s, part(c_ref.at[1], 0))
    north_west = clean(no_n, part(c_ref.at[2], 1))
    north_east = clean(no_n, part(c_ref.at[3], 0))

    def turned(values, shift):
        shift %= LANES
        return pltpu.roll(values, shift, 1) if shift else values

    def join(up, below, start):
        return jnp.where(
            lane < 4, turned(up, -start),
            jnp.where(lane >= LANES - 4, turned(below, LANES - 4 - start), 0.0),
        )

    for i in range(count):
        if i < 4:
            up, below, at = north_west, south_west, i
        elif i < 4 + lon_cells:
            col = i - 4
            up, below, at = north[col // 32], south[col // 32], col % 32
        else:
            up, below, at = north_east, south_east, i - 4 - lon_cells
        xa[i, :, lat_cells:wide] = join(up, below, 4 * at)

    south_k, north_k = clean(no_s, part(p_ref.at[0], 2)), clean(no_n, part(p_ref.at[1], 2))
    tail_col = (lon_cells // 8) * 8
    corners = (
        (pltpu.roll(clean(no_n, part(c_ref.at[2], 0)), 4, 0), pltpu.roll(clean(no_s, part(c_ref.at[0], 0)), 4, 0)),
        (pltpu.roll(clean(no_n, part(c_ref.at[3], 1)), 4, 0), pltpu.roll(clean(no_s, part(c_ref.at[1], 1)), 4, 0)),
    )
    for which, ref in enumerate((kx, dx)):
        from_west = join(corners[0][0], corners[0][1], tail_col + 4 * which)
        ref[0:8, lat_cells:wide] = jnp.where(sublane >= 4, from_west, 0.0)
        for j in range((tall - 8) // 8):
            piece = join(north_k, south_k, 8 * j + 4 * which)
            if 8 * j == tail_col:
                piece = jnp.where(sublane < 4, piece, join(corners[1][0], corners[1][1], 4 * which))
            ref[8 + 8 * j : 16 + 8 * j, lat_cells:wide] = piece

    @pl.when(is_top)
    def _():
        fold_strip(n_lon, lon_cells, b, q_ref, fp_ref, ghost_ref, coast_ref)
        for which, ref in enumerate((kx, dx)):
            for j in range(tall // 8):
                at = slice(8 * j, 8 * j + 8)
                ref[at, lat_cells:wide] = jnp.where(
                    lane == 0, coast_ref[which, at, :], ref[at, lat_cells:wide]
                )

    for j in range(tall // 8):
        at = slice(8 * j, 8 * j + 8)
        k0, d0 = kx[at, :], dx[at, :]
        lat_k[at, :] = k0 * pltpu.roll(k0, wide - 1, 1)
        lat_d[at, :] = jnp.minimum(d0, pltpu.roll(d0, wide - 1, 1))
        if j < tall // 8 - 1:
            after = slice(8 * j + 1, 8 * j + 9)
            lon_k[at, :] = k0 * kx[after, :]
            lon_d[at, :] = jnp.minimum(d0, dx[after, :])
        else:
            after = slice(8 * j + 1, 8 * j + 8)
            at = slice(8 * j, 8 * j + 7)
            lon_k[at, :] = kx[at, :] * kx[after, :]
            lon_d[at, :] = jnp.minimum(dx[at, :], dx[after, :])
            lon_k[tall - 1 : tall, :] = jnp.zeros((1, wide), jnp.float32)
            lon_d[tall - 1 : tall, :] = jnp.zeros((1, wide), jnp.float32)

    level = (lax.broadcasted_iota(jnp.int32, (8, wide), 0) % 4).astype(jnp.float32)

    def row(ref, i):
        return jnp.broadcast_to(ref[pl.ds(i + 4, 1), :], (8, ref.shape[1]))

    def make_faces(i, carry):
        e_face[i] = jnp.where(row(lon_d, i) > level, row(lon_k, i), 0.0)
        n_face[i] = jnp.where(row(lat_d, i) > level, row(lat_k, i), 0.0)
        return carry

    lax.fori_loop(0, count, make_faces, 0, unroll=4)

    for copy in large:
        copy.wait()

    def mask(i, carry):
        xa[i] = jnp.where(row(dx, i) > level, xa[i], 0.0)
        return carry

    lax.fori_loop(0, count, mask, 0, unroll=4)

    def advance(source, i, state):
        x, flux_west = state
        x_east = source[i + 1]
        flux_east = e_face[i] * (x_east - x)
        flux_north = n_face[i] * (pltpu.roll(x, wide - 1, 1) - x)
        fresh = ((x + flux_east) - flux_west) + (flux_north - pltpu.roll(flux_north, 1, 1))
        return fresh, (x_east, flux_east)

    def refresh(ref, step):
        @pl.when(is_top)
        def _():
            ghosts = ghost_ref[step]
            for i in range(step + 1, count - step - 1):
                ref[i, :, lat_cells:wide] = jnp.where(
                    lane == 0, turned(ghosts, -i), ref[i, :, lat_cells:wide]
                )

    def start_of(source, first):
        x = source[first]
        return x, e_face[first - 1] * (x - source[first - 1])

    source, target = xa, xb
    for step in range(PASSES - 1):
        refresh(source, step)
        first, stop = step + 1, count - step - 1

        def one(i, state, source=source, target=target):
            fresh, state = advance(source, i, state)
            target[i] = fresh
            return state

        lax.fori_loop(first, stop, one, start_of(source, first), unroll=2)
        source, target = target, source
    refresh(source, PASSES - 1)

    short = lax.broadcasted_iota(jnp.int32, (8, lat_cells), 0)
    sigma = jnp.zeros((8, lat_cells), jnp.float32)
    expand = jnp.zeros((8, lat_cells), jnp.float32)
    for c in range(2):
        for k in range(4):
            sigma = jnp.where(short == 4 * c + k, sigma_ref[c, k], sigma)
            expand = jnp.where(short == 4 * c + k, expand_ref[c, k], expand)

    def balance(i, state):
        fresh, state = advance(source, i, state)
        scaled = sigma * fresh[:, 0:lat_cells]
        col = i - 4
        ratio = jnp.broadcast_to(ratio_ref[pl.ds(col, 1), :], (8, lat_cells))
        result = scaled + jnp.where(short >= 4, ratio * pltpu.roll(scaled, 4, 0), 0.0)
        ya[col] = result
        height_ref[pl.ds(col, 1), :] = elev_ref[pl.ds(col, 1), :] + jnp.sum(
            expand * result, axis=0, keepdims=True
        )
        return state

    state = start_of(source, 4)
    middle = (lon_cells // 4) * 2
    bounds = (0, middle, lon_cells)
    outs = []
    for chunk in range(2):
        lo, hi = bounds[chunk], bounds[chunk + 1]
        state = lax.fori_loop(lo + 4, hi + 4, balance, state, unroll=2)
        for c in range(2):
            copy = pltpu.make_async_copy(
                ya.at[pl.ds(lo, hi - lo), pl.ds(4 * c, 4), :],
                state_hbm.at[c, pl.ds(lo, hi - lo)],
                out_sems.at[2 * chunk + c],
            )
            copy.start()
            outs.append(copy)
    for copy in outs:
        copy.wait()


def local(
    n_lon, n_lat,
    control_fields,
    unexplained_elevation,
    diffusivity,
    depth_levels,
    fold_partner,
    prior_sigmas,
    haline_thermal_ratio,
    expansion_coefficients,
):
    levels, lon_cells, lat_cells = control_fields.shape[1:]
    fields = control_fields.transpose(0, 2, 1, 3)
    partners = jnp.pad(
        fold_partner.reshape(n_lon, lon_cells), ((0, 0), (0, LANES - lon_cells))
    )
    tall = -(-lon_cells // 8) * 8 + 8
    count = lon_cells + 8
    wide = lat_cells + LANES
    f32 = jnp.float32
    vmem = pl.BlockSpec(memory_space=pltpu.VMEM)
    smem = pl.BlockSpec(memory_space=pltpu.SMEM)
    anywhere = pl.BlockSpec(memory_space=pl.ANY)
    halo_shapes = (
        (2, 2, 4, levels, lat_cells),
        (2, 8, lat_cells),
        (2, 8, 4 * LANES),
        (4, 8, 2 * LANES),
        (10, 8, 4 * LANES),
    )
    halos = pl.pallas_call(
        functools.partial(exchange_kernel, n_lon, n_lat),
        name="exchange",
        out_shape=tuple(jax.ShapeDtypeStruct(shape, f32) for shape in halo_shapes),
        in_specs=[anywhere, vmem, vmem],
        out_specs=(anywhere,) * 5,
        scratch_shapes=[
            pltpu.VMEM((2, lon_cells, 8, LANES), f32),
            pltpu.VMEM((8, LANES), f32),
            pltpu.VMEM((2, 8, lat_cells), f32),
            pltpu.VMEM((2, 8, 4 * LANES), f32),
            pltpu.SemaphoreType.DMA((20,)),
            pltpu.SemaphoreType.DMA((20,)),
            pltpu.SemaphoreType.DMA((10,)),
            pltpu.SemaphoreType.DMA((4,)),
        ],
        compiler_params=pltpu.CompilerParams(
            collective_id=0, has_side_effects=True, vmem_limit_bytes=40 * 1024 * 1024
        ),
    )(fields, diffusivity, depth_levels)
    state, height = pl.pallas_call(
        functools.partial(compute_kernel, n_lon, n_lat),
        name="diffuse",
        out_shape=(
            jax.ShapeDtypeStruct(fields.shape, f32),
            jax.ShapeDtypeStruct((lon_cells, lat_cells), f32),
        ),
        in_specs=[anywhere] + [vmem] * 5 + [smem] * 2 + [anywhere] * 5,
        out_specs=(anywhere, vmem),
        scratch_shapes=[
            pltpu.VMEM((count, 8, wide), f32),
            pltpu.VMEM((count, 8, wide), f32),
            pltpu.VMEM((lon_cells, 8, lat_cells), f32),
        ]
        + [pltpu.VMEM((tall, wide), f32)] * 6
        + [pltpu.VMEM((count, 8, wide), f32)] * 2
        + [pltpu.VMEM(shape, f32) for shape in halo_shapes[1:]]
        + [
            pltpu.VMEM((PASSES, 8, LANES), f32),
            pltpu.VMEM((2, LANES + 8, LANES), f32),
            pltpu.SemaphoreType.DMA((10,)),
            pltpu.SemaphoreType.DMA((4,)),
        ],
        compiler_params=pltpu.CompilerParams(vmem_limit_bytes=48 * 1024 * 1024),
    )(
        fields, unexplained_elevation, diffusivity, depth_levels, haline_thermal_ratio,
        partners, prior_sigmas, expansion_coefficients, *halos,
    )
    return state.transpose(0, 2, 1, 3), height


def solution(mesh):
    return jax.shard_map(
        functools.partial(local, mesh.shape["lon"], mesh.shape["lat"]),
        mesh=mesh,
        in_specs=(
            P(None, None, "lon", "lat"),
            P("lon", "lat"),
            P("lon", "lat"),
            P("lon", "lat"),
            P(),
            P(),
            P("lon", "lat"),
            P(),
        ),
        out_specs=(P(None, None, "lon", "lat"), P("lon", "lat")),
        check_vma=False,
    )
```

time: 27.1 us -> 43.6 us (1.61)
  Pallas kernels: 17.9 us -> 36.2 us
  local copies, waits for them, and re-layouts: 7.44 us -> 6.15 us
  other arithmetic: 0.7 us -> 0 us
    pallas_call x1, Pallas kernels: 6.19 us -> 25.6 us  [local(): pl.pallas_call(functools.partial(compute_kernel, n_lon, n_lat), name='dif...]
    unnamed x24 -> x20, local copies, waits for them, and re-layouts: 7.36 us -> 5.38 us
    pallas_call x1, Pallas kernels: 11.7 us -> 10.6 us  [local(): pl.pallas_call(functools.partial(exchange_kernel, n_lon, n_lat), name='ex...]
    select_n x1 -> x0, other arithmetic: 0.7 us -> none  [local(): fold_partner % lon_cells]
    reshape x1, local copies, waits for them, and re-layouts: 0.08 us -> 0.76 us  [local(): fold_partner.reshape(n_lon, lon_cells)]
where the time goes in v2:
time: 43.6 us; the launch traced here: 43 us
  Pallas kernels  36.2 us (83%)
  local copies, waits for them, and re-layouts  6.15 us (14%)
  between operations  0.7 us (2%)
    pallas_call x1, Pallas kernels, local(): pl.pallas_call(functools.partial(compute_kernel, n_lon, n_lat), name='dif...  25.6 us
    pallas_call x1, Pallas kernels, local(): pl.pallas_call(functools.partial(exchange_kernel, n_lon, n_lat), name='ex...  10.6 us
    unnamed x20, local copies, waits for them, and re-layouts  5.38 us

profile of v2, /device:TPU:1, one launch (start us, length us, event | category | flops | bytes accessed | tf_op | source)
XLA Modules:
  0.0 43.0 jit_solution(15783724494705572980)
XLA Ops:
  0.6 0.8 %reshape.7 = s32[8,68]{1,0:T(8,128)S(1)} reshape(s32[544]{0:T(1024)} %param.12) | data formatting | bytes 4352 | tf_op jit(solution)/shard_map/reshape | solution.py:583
  1.4 0.0 copy-start
  1.4 1.1 %copy-done = f32[2,4,68,384]{3,1,2,0:T(4,128)S(1)} copy-done((f32[2,4,68,384]{3,1,2,0:T(4,128)S(1)}, f32[2,4,68,384]{3,1,2,0:T(4,128)}, u32[]{:S(2)}) %copy-start) | copy-done | bytes 835608
  2.6 0.0 copy-start.2
  2.6 0.9 %copy-done.2 = f32[68,384]{1,0:T(8,128)S(1)} copy-done((f32[68,384]{1,0:T(8,128)S(1)}, f32[68,384]{1,0:T(8,128)}, u32[]{:S(2)}) %copy-start.2) | copy-done | bytes 104472
  3.5 0.0 copy-start.4
  3.5 0.9 %copy-done.4 = s32[68,384]{1,0:T(8,128)S(1)} copy-done((s32[68,384]{1,0:T(8,128)S(1)}, s32[68,384]{1,0:T(8,128)}, u32[]{:S(2)}) %copy-start.4) | copy-done | bytes 104472
  4.3 0.0 copy-start.1
  4.3 0.0 copy-start.3
  4.4 0.0 copy-start.5
  4.4 0.0 copy-start.9
  4.4 10.6 %exchange.1 = (f32[2,2,4,4,384]{4,3,2,1,0:T(4,128)S(1)}, f32[2,8,384]{2,1,0:T(8,128)S(1)}, f32[2,8,512]{2,1,0:T(8,128)S(1)}, f32[4,8,256]{2,1,0:T(8,128)S(1)}, f32[10,8,512]{2,1,0:T(8,128)S(1)}) custom-call(f32[2,68,4,384]{3,2,1,0:T(4,128)S(1)} %bitcast.2, f32[68,384]{1,0:T(8,128)S(1)} %copy-done.2, s32[68,384]{1,0:T(8,128)S(1)} %copy-done.4), custom_call_target="tpu_custom_call" | custom-call | tf_op jit(solution)/shard_map/exchange/pallas_call | solution.py:599
  15.0 0.0 copy-start.8
  15.0 0.0 copy-done.1
  15.0 0.0 copy-done.3
  15.0 0.0 copy-done.5
  15.0 0.0 copy-done.9
  15.0 0.6 %copy-done.8 = f32[2,4]{1,0:T(2,128)S(1)} copy-done((f32[2,4]{1,0:T(2,128)S(1)}, f32[2,4]{1,0:T(2,128)}, u32[]{:S(2)}) %copy-start.8) | copy-done | bytes 56
  15.7 0.0 copy-start.6
  15.7 0.9 %copy-done.6 = f32[68,384]{1,0:T(8,128)S(1)} copy-done((f32[68,384]{1,0:T(8,128)S(1)}, f32[68,384]{1,0:T(8,128)}, u32[]{:S(2)}) %copy-start.6) | copy-done | bytes 104472
  16.6 0.0 copy-start.7
  16.6 0.9 %copy-done.7 = f32[68,384]{1,0:T(8,128)S(1)} copy-done((f32[68,384]{1,0:T(8,128)S(1)}, f32[68,384]{1,0:T(8,128)}, u32[]{:S(2)}) %copy-start.7) | copy-done | bytes 104472
  17.5 25.6 %diffuse.1 = (f32[2,68,4,384]{3,2,1,0:T(4,128)}, f32[68,384]{1,0:T(8,128)}) custom-call(f32[2,68,4,384]{3,2,1,0:T(4,128)S(1)} %bitcast.3, f32[68,384]{1,0:T(8,128)S(1)} %copy-done.6, f32[68,384]{1,0:T(8,128)S(1)} %copy-done.3, s32[68,384]{1,0:T(8,128)S(1)} %copy-done.5, f32[68,384]{1,0:T(8,128)S(1)} %copy-done.7, s32[8,128]{1,0:T(8,128)S(1)} %pad.4.fp_ref, ...), custom_call_target="tpu_custom_call" | custom-call | tf_op jit(solution)/shard_map/diffuse/pallas_call | solution.py:619
  (1 shorter events, 0.0 us)
Async XLA Ops:
  1.4 1.2 %copy-start = (f32[2,4,68,384]{3,1,2,0:T(4,128)S(1)}, f32[2,4,68,384]{3,1,2,0:T(4,128)}, u32[]{:S(2)}) copy-start(f32[2,4,68,384]{3,1,2,0:T(4,128)} %param.8) | copy-start | bytes 2506756
  2.6 0.9 %copy-start.2 = (f32[68,384]{1,0:T(8,128)S(1)}, f32[68,384]{1,0:T(8,128)}, u32[]{:S(2)}) copy-start(f32[68,384]{1,0:T(8,128)} %k_ref.3) | copy-start | bytes 313348
  3.5 0.9 %copy-start.4 = (s32[68,384]{1,0:T(8,128)S(1)}, s32[68,384]{1,0:T(8,128)}, u32[]{:S(2)}) copy-start(s32[68,384]{1,0:T(8,128)} %d_ref.3) | copy-start | bytes 313348
  4.3 10.7 %copy-start.1 = (f32[2,4,68,384]{3,1,2,0:T(4,128)S(1)}, f32[2,4,68,384]{3,1,2,0:T(4,128)}, u32[]{:S(2)}) copy-start(f32[2,4,68,384]{3,1,2,0:T(4,128)} %param.8) | copy-start | bytes 2506756
  4.3 10.7 %copy-start.3 = (f32[68,384]{1,0:T(8,128)S(1)}, f32[68,384]{1,0:T(8,128)}, u32[]{:S(2)}) copy-start(f32[68,384]{1,0:T(8,128)} %k_ref.3) | copy-start | bytes 313348
  4.4 10.7 %copy-start.5 = (s32[68,384]{1,0:T(8,128)S(1)}, s32[68,384]{1,0:T(8,128)}, u32[]{:S(2)}) copy-start(s32[68,384]{1,0:T(8,128)} %d_ref.3) | copy-start | bytes 313348
  4.4 10.7 %copy-start.9 = (f32[2,4]{1,0:T(2,128)S(1)}, f32[2,4]{1,0:T(2,128)}, u32[]{:S(2)}) copy-start(f32[2,4]{1,0:T(2,128)} %expand_ref.1) | copy-start | bytes 100
  15.0 0.7 %copy-start.8 = (f32[2,4]{1,0:T(2,128)S(1)}, f32[2,4]{1,0:T(2,128)}, u32[]{:S(2)}) copy-start(f32[2,4]{1,0:T(2,128)} %sigma_ref.1) | copy-start | bytes 100
  15.7 0.9 %copy-start.6 = (f32[68,384]{1,0:T(8,128)S(1)}, f32[68,384]{1,0:T(8,128)}, u32[]{:S(2)}) copy-start(f32[68,384]{1,0:T(8,128)} %elev_ref.1) | copy-start | bytes 313348
  16.6 0.9 %copy-start.7 = (f32[68,384]{1,0:T(8,128)S(1)}, f32[68,384]{1,0:T(8,128)}, u32[]{:S(2)}) copy-start(f32[68,384]{1,0:T(8,128)} %ratio_ref.1) | copy-start | bytes 313348

commit v3 on v2

--- a/solution.py
+++ b/solution.py
@@ -15,11 +15,15 @@
 MESH = pl.DeviceIdType.MESH
 
 
+def unroll_of(trips):
+    return max(k for k in range(1, 38) if trips % k == 0)
+
+
 def exchange_kernel(
     n_lon, n_lat,
-    f_ref, k_ref, d_ref,
+    f_ref, k_hbm, d_hbm,
     ew_out, kd_out, p_out, c_out, q_out,
-    edge_buf, tail_buf, kd_buf, p_buf, send_sem, recv_sem, local_sem, load_sem,
+    k_ref, d_ref, edge_buf, tail_buf, kd_buf, p_buf, send_sem, recv_sem, local_sem, load_sem,
 ):
     lon_cells, lat_cells = k_ref.shape
     b = lax.axis_index("lon")
@@ -41,7 +45,11 @@
         for side, start in ((0, lat_cells - LANES), (1, 0))
         for c in range(2)
     ]
-    for copy in loads:
+    bases = [
+        pltpu.make_async_copy(k_hbm, k_ref, load_sem.at[4]),
+        pltpu.make_async_copy(d_hbm, d_ref, load_sem.at[5]),
+    ]
+    for copy in bases + loads:
         copy.start()
 
     straight = [
@@ -102,6 +110,8 @@
     for copy in far:
         copy.start()
 
+    for copy in bases:
+        copy.wait()
     for source, start in ((k_ref, 0), (d_ref, 4)):
         kd_buf[0, start : start + 4, :] = source[lon_cells - 4 : lon_cells, :].astype(jnp.float32)
         kd_buf[1, start : start + 4, :] = source[0:4, :].astype(jnp.float32)
@@ -346,10 +356,10 @@
 
 def compute_kernel(
     n_lon, n_lat,
-    f_ref, elev_ref, k_ref, d_ref, ratio_ref, fp_ref, sigma_ref, expand_ref,
+    f_ref, elev_hbm, k_hbm, d_hbm, ratio_hbm, fp_ref, sigma_hbm, expand_hbm,
     ew_hbm, kd_hbm, p_hbm, c_hbm, q_hbm,
     state_hbm, height_ref,
-    xa, xb, ya, kx, dx, lon_k, lon_d, lat_k, lat_d, e_face, n_face,
+    elev_ref, k_ref, d_ref, ratio_ref, sigma_ref, expand_ref, xa, xb, ya, kx, dx, lon_k, lon_d, lat_k, lat_d, e_face, n_face,
     kd_ref, p_ref, c_ref, q_ref, ghost_ref, coast_ref, sems, out_sems,
 ):
     lon_cells, lat_cells = k_ref.shape
@@ -378,11 +388,23 @@
             ),
             pltpu.make_async_copy(f_ref.at[c], xa.at[pl.ds(4, lon_cells), half, own], sems.at[8 + c]),
         ]
-    for copy in small + large:
+    base = [
+        pltpu.make_async_copy(k_hbm, k_ref, sems.at[10]),
+        pltpu.make_async_copy(d_hbm, d_ref, sems.at[11]),
+    ]
+    late = [
+        pltpu.make_async_copy(elev_hbm, elev_ref, sems.at[12]),
+        pltpu.make_async_copy(ratio_hbm, ratio_ref, sems.at[13]),
+        pltpu.make_async_copy(sigma_hbm, sigma_ref, sems.at[14]),
+        pltpu.make_async_copy(expand_hbm, expand_ref, sems.at[15]),
+    ]
+    for copy in base + small + large + late:
         copy.start()
 
     sublane = lax.broadcasted_iota(jnp.int32, (8, LANES), 0)
     lane = lax.broadcasted_iota(jnp.int32, (8, LANES), 1)
+    for copy in base:
+        copy.wait()
     for ref, source in ((kx, k_ref), (dx, d_ref)):
         ref[0:8, :] = jnp.zeros((8, wide), jnp.float32)
         ref[8 : 8 + lon_cells, 0:lat_cells] = source[...].astype(jnp.float32)
@@ -481,7 +503,7 @@
         n_face[i] = jnp.where(row(lat_d, i) > level, row(lat_k, i), 0.0)
         return carry
 
-    lax.fori_loop(0, count, make_faces, 0, unroll=4)
+    lax.fori_loop(0, count, make_faces, 0, unroll=unroll_of(count))
 
     for copy in large:
         copy.wait()
@@ -490,7 +512,7 @@
         xa[i] = jnp.where(row(dx, i) > level, xa[i], 0.0)
         return carry
 
-    lax.fori_loop(0, count, mask, 0, unroll=4)
+    lax.fori_loop(0, count, mask, 0, unroll=unroll_of(count))
 
     def advance(source, i, state):
         x, flux_west = state
@@ -523,10 +545,12 @@
             target[i] = fresh
             return state
 
-        lax.fori_loop(first, stop, one, start_of(source, first), unroll=2)
+        lax.fori_loop(first, stop, one, start_of(source, first), unroll=unroll_of(stop - first))
         source, target = target, source
     refresh(source, PASSES - 1)
 
+    for copy in late:
+        copy.wait()
     short = lax.broadcasted_iota(jnp.int32, (8, lat_cells), 0)
     sigma = jnp.zeros((8, lat_cells), jnp.float32)
     expand = jnp.zeros((8, lat_cells), jnp.float32)
@@ -553,7 +577,7 @@
     outs = []
     for chunk in range(2):
         lo, hi = bounds[chunk], bounds[chunk + 1]
-        state = lax.fori_loop(lo + 4, hi + 4, balance, state, unroll=2)
+        state = lax.fori_loop(lo + 4, hi + 4, balance, state, unroll=unroll_of((hi - lo) // 2))
         for c in range(2):
             copy = pltpu.make_async_copy(
                 ya.at[pl.ds(lo, hi - lo), pl.ds(4 * c, 4), :],
@@ -587,7 +611,7 @@
     wide = lat_cells + LANES
     f32 = jnp.float32
     vmem = pl.BlockSpec(memory_space=pltpu.VMEM)
-    smem = pl.BlockSpec(memory_space=pltpu.SMEM)
+    hbm = pl.BlockSpec(memory_space=pltpu.HBM)
     anywhere = pl.BlockSpec(memory_space=pl.ANY)
     halo_shapes = (
         (2, 2, 4, levels, lat_cells),
@@ -600,9 +624,11 @@
         functools.partial(exchange_kernel, n_lon, n_lat),
         name="exchange",
         out_shape=tuple(jax.ShapeDtypeStruct(shape, f32) for shape in halo_shapes),
-        in_specs=[anywhere, vmem, vmem],
+        in_specs=[hbm] * 3,
         out_specs=(anywhere,) * 5,
         scratch_shapes=[
+            pltpu.VMEM((lon_cells, lat_cells), f32),
+            pltpu.VMEM((lon_cells, lat_cells), jnp.int32),
             pltpu.VMEM((2, lon_cells, 8, LANES), f32),
             pltpu.VMEM((8, LANES), f32),
             pltpu.VMEM((2, 8, lat_cells), f32),
@@ -610,10 +636,10 @@
             pltpu.SemaphoreType.DMA((20,)),
             pltpu.SemaphoreType.DMA((20,)),
             pltpu.SemaphoreType.DMA((10,)),
-            pltpu.SemaphoreType.DMA((4,)),
+            pltpu.SemaphoreType.DMA((6,)),
         ],
         compiler_params=pltpu.CompilerParams(
-            collective_id=0, has_side_effects=True, vmem_limit_bytes=40 * 1024 * 1024
+            collective_id=0, has_side_effects=True, vmem_limit_bytes=63 * 1024 * 1024
         ),
     )(fields, diffusivity, depth_levels)
     state, height = pl.pallas_call(
@@ -623,9 +649,15 @@
             jax.ShapeDtypeStruct(fields.shape, f32),
             jax.ShapeDtypeStruct((lon_cells, lat_cells), f32),
         ),
-        in_specs=[anywhere] + [vmem] * 5 + [smem] * 2 + [anywhere] * 5,
+        in_specs=[hbm] * 5 + [vmem] + [hbm] * 2 + [anywhere] * 5,
         out_specs=(anywhere, vmem),
         scratch_shapes=[
+            pltpu.VMEM((lon_cells, lat_cells), f32),
+            pltpu.VMEM((lon_cells, lat_cells), f32),
+            pltpu.VMEM((lon_cells, lat_cells), jnp.int32),
+            pltpu.VMEM((lon_cells, lat_cells), f32),
+            pltpu.SMEM((2, levels), f32),
+            pltpu.SMEM((2, levels), f32),
             pltpu.VMEM((count, 8, wide), f32),
             pltpu.VMEM((count, 8, wide), f32),
             pltpu.VMEM((lon_cells, 8, lat_cells), f32),
@@ -636,10 +668,10 @@
         + [
             pltpu.VMEM((PASSES, 8, LANES), f32),
             pltpu.VMEM((2, LANES + 8, LANES), f32),
-            pltpu.SemaphoreType.DMA((10,)),
+            pltpu.SemaphoreType.DMA((16,)),
             pltpu.SemaphoreType.DMA((4,)),
         ],
-        compiler_params=pltpu.CompilerParams(vmem_limit_bytes=48 * 1024 * 1024),
+        compiler_params=pltpu.CompilerParams(vmem_limit_bytes=63 * 1024 * 1024),
     )(
         fields, unexplained_elevation, diffusivity, depth_levels, haline_thermal_ratio,
         partners, prior_sigmas, expansion_coefficients, *halos,

time: 43.6 us -> 28.7 us (0.66)
  Pallas kernels: 36.2 us -> 26.3 us
  local copies, waits for them, and re-layouts: 6.15 us -> 1.35 us
    pallas_call x1, Pallas kernels: 25.6 us -> 15.4 us  [local(): pl.pallas_call(functools.partial(compute_kernel, n_lon, n_lat), name='dif...]
    unnamed x20 -> x0, local copies, waits for them, and re-layouts: 5.38 us -> none
    pad x1, local copies, waits for them, and re-layouts: 0.01 us -> 0.59 us  [local(): jnp.pad(fold_partner.reshape(n_lon, lon_cells), ((0, 0), (0, LANES - lon_...]
where the time goes in v3:
time: 28.7 us; the launch traced here: 28.2 us
  Pallas kernels  26.3 us (92%)
  local copies, waits for them, and re-layouts  1.35 us (5%)
  between operations  0.64 us (2%)
    pallas_call x1, Pallas kernels, local(): pl.pallas_call(functools.partial(compute_kernel, n_lon, n_lat), name='dif...  15.4 us
    pallas_call x1, Pallas kernels, local(): pl.pallas_call(functools.partial(exchange_kernel, n_lon, n_lat), name='ex...  10.8 us
    reshape x1, local copies, waits for them, and re-layouts, local(): fold_partner.reshape(n_lon, lon_cells)  0.76 us
    pad x1, local copies, waits for them, and re-layouts, local(): jnp.pad(fold_partner.reshape(n_lon, lon_cells), ((0, 0), (0, LANES - lon_...  0.59 us

profile of v3, /device:TPU:1, one launch (start us, length us, event | category | flops | bytes accessed | tf_op | source)
XLA Modules:
  0.0 28.2 jit_solution(10478498651401771044)
XLA Ops:
  0.6 0.8 %reshape.7 = s32[8,68]{1,0:T(8,128)S(1)} reshape(s32[544]{0:T(1024)} %param.12) | data formatting | bytes 4352 | tf_op jit(solution)/shard_map/reshape | solution.py:607
  1.4 0.6 %pad.4.fp_ref = s32[8,128]{1,0:T(8,128)} pad(s32[8,68]{1,0:T(8,128)S(1)} %reshape.7, s32[]{:T(128)} %constant.0.clone.1), padding=0_0x0_60 | pad | bytes 6276 | tf_op jit(solution)/shard_map/jit(_pad)/pad | solution.py:606
  2.0 10.8 %exchange.1 = (f32[2,2,4,4,384]{4,3,2,1,0:T(4,128)}, f32[2,8,384]{2,1,0:T(8,128)}, f32[2,8,512]{2,1,0:T(8,128)}, f32[4,8,256]{2,1,0:T(8,128)}, f32[10,8,512]{2,1,0:T(8,128)}) custom-call(f32[2,68,4,384]{3,2,1,0:T(4,128)} %bitcast.2, f32[68,384]{1,0:T(8,128)} %k_hbm.3, s32[68,384]{1,0:T(8,128)} %d_hbm.3), custom_call_target="tpu_custom_call" | custom-call | tf_op jit(solution)/shard_map/exchange/pallas_call | solution.py:623
  12.8 15.4 %diffuse.1 = (f32[2,68,4,384]{3,2,1,0:T(4,128)}, f32[68,384]{1,0:T(8,128)}) custom-call(f32[2,68,4,384]{3,2,1,0:T(4,128)} %bitcast.3, f32[68,384]{1,0:T(8,128)} %elev_hbm.1, f32[68,384]{1,0:T(8,128)} %k_hbm.3, s32[68,384]{1,0:T(8,128)} %d_hbm.3, f32[68,384]{1,0:T(8,128)} %ratio_hbm.1, s32[8,128]{1,0:T(8,128)} %pad.4.fp_ref, f32[2,4]{1,0:T(2,128)} %sigma_hbm.1, ...), custom_call_target="tpu_custom_call" | custom-call | tf_op jit(solution)/shard_map/diffuse/pallas_call | solution.py:645

commit v4 on v3

--- a/solution.py
+++ b/solution.py
@@ -15,8 +15,10 @@
 MESH = pl.DeviceIdType.MESH
 
 
-def unroll_of(trips):
-    return max(k for k in range(1, 38) if trips % k == 0)
+def unrolled(first, stop, body, state):
+    for i in range(first, stop):
+        state = body(i, state)
+    return state
 
 
 def exchange_kernel(
@@ -359,7 +361,7 @@
     f_ref, elev_hbm, k_hbm, d_hbm, ratio_hbm, fp_ref, sigma_hbm, expand_hbm,
     ew_hbm, kd_hbm, p_hbm, c_hbm, q_hbm,
     state_hbm, height_ref,
-    elev_ref, k_ref, d_ref, ratio_ref, sigma_ref, expand_ref, xa, xb, ya, kx, dx, lon_k, lon_d, lat_k, lat_d, e_face, n_face,
+    elev_ref, k_ref, d_ref, ratio_ref, sigma_ref, expand_ref, xa, xb, raw, ew_ref, kx, dx, lon_k, lon_d, lat_k, lat_d, e_face, n_face,
     kd_ref, p_ref, c_ref, q_ref, ghost_ref, coast_ref, sems, out_sems,
 ):
     lon_cells, lat_cells = k_ref.shape
@@ -377,17 +379,10 @@
         pltpu.make_async_copy(c_hbm, c_ref, sems.at[2]),
         pltpu.make_async_copy(q_hbm, q_ref, sems.at[3]),
     ]
-    large = []
-    for c in range(2):
-        half = pl.ds(4 * c, 4)
-        own = pl.ds(0, lat_cells)
-        large += [
-            pltpu.make_async_copy(ew_hbm.at[0, c], xa.at[pl.ds(0, 4), half, own], sems.at[4 + c]),
-            pltpu.make_async_copy(
-                ew_hbm.at[1, c], xa.at[pl.ds(lon_cells + 4, 4), half, own], sems.at[6 + c]
-            ),
-            pltpu.make_async_copy(f_ref.at[c], xa.at[pl.ds(4, lon_cells), half, own], sems.at[8 + c]),
-        ]
+    large = [
+        pltpu.make_async_copy(ew_hbm, ew_ref, sems.at[4]),
+        pltpu.make_async_copy(f_ref, raw, sems.at[5]),
+    ]
     base = [
         pltpu.make_async_copy(k_hbm, k_ref, sems.at[10]),
         pltpu.make_async_copy(d_hbm, d_ref, sems.at[11]),
@@ -503,16 +498,26 @@
         n_face[i] = jnp.where(row(lat_d, i) > level, row(lat_k, i), 0.0)
         return carry
 
-    lax.fori_loop(0, count, make_faces, 0, unroll=unroll_of(count))
+    unrolled(0, count, make_faces, 0)
 
     for copy in large:
         copy.wait()
 
-    def mask(i, carry):
-        xa[i] = jnp.where(row(dx, i) > level, xa[i], 0.0)
+    def mask(i, where_from):
+        wet = row(dx, i) > level
+        pair = jnp.concatenate([where_from[0], where_from[1]], axis=0)
+        xa[i, :, 0:lat_cells] = jnp.where(wet[:, 0:lat_cells], pair, 0.0)
+        xa[i, :, lat_cells:wide] = jnp.where(wet[:, lat_cells:wide], xa[i, :, lat_cells:wide], 0.0)
+
+    for i in range(4):
+        mask(i, (ew_ref[0, 0, i], ew_ref[0, 1, i]))
+        mask(lon_cells + 4 + i, (ew_ref[1, 0, i], ew_ref[1, 1, i]))
+
+    def mask_own(col, carry):
+        mask(col + 4, (raw[0, col], raw[1, col]))
         return carry
 
-    lax.fori_loop(0, count, mask, 0, unroll=unroll_of(count))
+    unrolled(0, lon_cells, mask_own, 0)
 
     def advance(source, i, state):
         x, flux_west = state
@@ -545,7 +550,7 @@
             target[i] = fresh
             return state
 
-        lax.fori_loop(first, stop, one, start_of(source, first), unroll=unroll_of(stop - first))
+        unrolled(first, stop, one, start_of(source, first))
         source, target = target, source
     refresh(source, PASSES - 1)
 
@@ -565,7 +570,8 @@
         col = i - 4
         ratio = jnp.broadcast_to(ratio_ref[pl.ds(col, 1), :], (8, lat_cells))
         result = scaled + jnp.where(short >= 4, ratio * pltpu.roll(scaled, 4, 0), 0.0)
-        ya[col] = result
+        raw[0, col] = result[0:4]
+        raw[1, col] = result[4:8]
         height_ref[pl.ds(col, 1), :] = elev_ref[pl.ds(col, 1), :] + jnp.sum(
             expand * result, axis=0, keepdims=True
         )
@@ -577,15 +583,13 @@
     outs = []
     for chunk in range(2):
         lo, hi = bounds[chunk], bounds[chunk + 1]
-        state = lax.fori_loop(lo + 4, hi + 4, balance, state, unroll=unroll_of((hi - lo) // 2))
-        for c in range(2):
-            copy = pltpu.make_async_copy(
-                ya.at[pl.ds(lo, hi - lo), pl.ds(4 * c, 4), :],
-                state_hbm.at[c, pl.ds(lo, hi - lo)],
-                out_sems.at[2 * chunk + c],
-            )
-            copy.start()
-            outs.append(copy)
+        state = unrolled(lo + 4, hi + 4, balance, state)
+        part_of = pl.ds(lo, hi - lo)
+        copy = pltpu.make_async_copy(
+            raw.at[:, part_of], state_hbm.at[:, part_of], out_sems.at[chunk]
+        )
+        copy.start()
+        outs.append(copy)
     for copy in outs:
         copy.wait()
 
@@ -660,7 +664,8 @@
             pltpu.SMEM((2, levels), f32),
             pltpu.VMEM((count, 8, wide), f32),
             pltpu.VMEM((count, 8, wide), f32),
-            pltpu.VMEM((lon_cells, 8, lat_cells), f32),
+            pltpu.VMEM(fields.shape, f32),
+            pltpu.VMEM(halo_shapes[0], f32),
         ]
         + [pltpu.VMEM((tall, wide), f32)] * 6
         + [pltpu.VMEM((count, 8, wide), f32)] * 2

time: 28.7 us -> 34.5 us (1.20)
  Pallas kernels: 26.3 us -> 32.1 us
    pallas_call x1, Pallas kernels: 15.4 us -> 21.2 us  [local(): pl.pallas_call(functools.partial(compute_kernel, n_lon, n_lat), name='dif...]
where the time goes in v4:
time: 34.5 us; the launch traced here: 34 us
  Pallas kernels  32.1 us (93%)
  local copies, waits for them, and re-layouts  1.35 us (4%)
  between operations  0.64 us (2%)
    pallas_call x1, Pallas kernels, local(): pl.pallas_call(functools.partial(compute_kernel, n_lon, n_lat), name='dif...  21.2 us
    pallas_call x1, Pallas kernels, local(): pl.pallas_call(functools.partial(exchange_kernel, n_lon, n_lat), name='ex...  10.8 us
    reshape x1, local copies, waits for them, and re-layouts, local(): fold_partner.reshape(n_lon, lon_cells)  0.76 us

profile of v4, /device:TPU:1, one launch (start us, length us, event | category | flops | bytes accessed | tf_op | source)
XLA Modules:
  0.0 34.0 jit_solution(5234470353298971683)
XLA Ops:
  0.6 0.8 %reshape.7 = s32[8,68]{1,0:T(8,128)S(1)} reshape(s32[544]{0:T(1024)} %param.12) | data formatting | bytes 4352 | tf_op jit(solution)/shard_map/reshape | solution.py:611
  1.4 0.6 %pad.4.fp_ref = s32[8,128]{1,0:T(8,128)} pad(s32[8,68]{1,0:T(8,128)S(1)} %reshape.7, s32[]{:T(128)} %constant.0.clone.1), padding=0_0x0_60 | pad | bytes 6276 | tf_op jit(solution)/shard_map/jit(_pad)/pad | solution.py:610
  2.0 10.8 %exchange.1 = (f32[2,2,4,4,384]{4,3,2,1,0:T(4,128)}, f32[2,8,384]{2,1,0:T(8,128)}, f32[2,8,512]{2,1,0:T(8,128)}, f32[4,8,256]{2,1,0:T(8,128)}, f32[10,8,512]{2,1,0:T(8,128)}) custom-call(f32[2,68,4,384]{3,2,1,0:T(4,128)} %bitcast.2, f32[68,384]{1,0:T(8,128)} %k_hbm.3, s32[68,384]{1,0:T(8,128)} %d_hbm.3), custom_call_target="tpu_custom_call" | custom-call | tf_op jit(solution)/shard_map/exchange/pallas_call | solution.py:627
  12.8 21.2 %diffuse.1 = (f32[2,68,4,384]{3,2,1,0:T(4,128)}, f32[68,384]{1,0:T(8,128)}) custom-call(f32[2,68,4,384]{3,2,1,0:T(4,128)} %bitcast.3, f32[68,384]{1,0:T(8,128)} %elev_hbm.1, f32[68,384]{1,0:T(8,128)} %k_hbm.3, s32[68,384]{1,0:T(8,128)} %d_hbm.3, f32[68,384]{1,0:T(8,128)} %ratio_hbm.1, s32[8,128]{1,0:T(8,128)} %pad.4.fp_ref, f32[2,4]{1,0:T(2,128)} %sigma_hbm.1, ...), custom_call_target="tpu_custom_call" | custom-call | tf_op jit(solution)/shard_map/diffuse/pallas_call | solution.py:649
